TPU v7x, 1024 devices: a whole 4x8x16 slice. The times are simulated.
1024 devices in a mesh: seq: 128 (over z, y), head: 8 (over x, core).
Axes of the slice: x: 4, y: 8, z: 16, core: 2. Of those that a mesh axis runs over, the one named last changes fastest.
Arguments:
- query_rows: bfloat16 [32, 32768, 128], P('head', 'seq'), may hold values from -6 to 6
- key_rows: bfloat16 [32, 32768, 128], P('head', 'seq'), may hold values from -0.5 to 0.5
- value_rows: bfloat16 [32, 32768, 128], P('head', 'seq'), may hold values from -40 to 40
- log_gate: float32 [32, 32768], P('head', 'seq'), may hold values from -1 to 0
- episode: int32 [32768], P('seq'), may hold values from 0 to 31, never falling along the last dimension, each value on 1 to 4096 neighbouring positions
- grad_out: bfloat16 [32, 32768, 128], P('head', 'seq'), may hold values from -6 to 6
Outputs:
- normed: bfloat16 [32, 32768, 128], P('head', 'seq')
- grad_query: bfloat16 [32, 32768, 128], P('head', 'seq')
- grad_key: bfloat16 [32, 32768, 128], P('head', 'seq')
- grad_value: bfloat16 [32, 32768, 128], P('head', 'seq')
Inputs may be any that keep to these rules, and one draw needn't show every extreme that they name: Episode ids never fall along the tokens; every episode spans 1 to 4096 tokens and one spans exactly 4096.
All inputs are finite; a program needn't handle non-finite values.
Results may differ from a plain program's by a relative error of at most 0.0062.
Values sent between devices are 32-bit elements; how exact they have to be, the bound alone decides.
No kernel may reach another device: no remote copies, remote signals or barrier semaphores. Data moves between devices by JAX's collectives and lax.ppermute only.
A program may use at most 32 MiB of HBM per device.

v0:
```python
import jax
import jax.numpy as jnp
from jax import lax
from jax.sharding import PartitionSpec as P

STRETCH = 256
REACH_MAX = 16


EPSILON = 1e-06


def passed_along(block, axis, distance):
    devices = range(lax.axis_size(axis))
    route = [(i - distance, i) for i in devices if i - distance in devices]
    return lax.ppermute(block, axis, route)


def from_everyone(value, axis):
    copies = jnp.broadcast_to(value, (lax.axis_size(axis), *value.shape))
    return lax.all_to_all(copies, axis, split_axis=0, concat_axis=0, tiled=True)


def of_everyone(value, axis):
    return from_everyone(value, axis).sum(axis=0)


def in_one(arrays, axis):
    ravelled, at, gathered = (jnp.concatenate([a.reshape(-1) for a in arrays]), 0, [])
    total = of_everyone(ravelled, axis)
    for a in arrays:
        gathered.append(total[at : at + a.size].reshape(a.shape))
        at += a.size
    return tuple(gathered)


def forward_join(earlier, latter):
    early_total, early_state, early_mark = earlier
    late_total, late_state, late_mark = latter
    empty_late = late_mark < 0
    carried = jnp.where(
        early_mark == late_mark, jnp.exp(late_total)[:, None, None] * early_state, 0.0
    )
    joined_state = jnp.where(empty_late, early_state, late_state + carried)
    joined_mark = jnp.where(empty_late, early_mark, late_mark)
    return (early_total + late_total, joined_state, joined_mark)


def reverse_merge_pass(earlier, latter):
    early_total, early_state, early_mark = earlier
    late_total, late_state, late_mark = latter
    empty_late = late_mark < 0
    carried = jnp.where(
        late_mark == early_mark, jnp.exp(late_total)[:, None, None] * early_state, 0.0
    )
    joined_state = jnp.where(empty_late, early_state, late_state + carried)
    joined_mark = jnp.where(empty_late, early_mark, late_mark)
    return (early_total + late_total, joined_state, joined_mark)


def shift_forward(payload, distance):
    return passed_along(payload, "seq", distance)


def shift_backward(payload, distance):
    return passed_along(payload, "seq", -distance)


def window_prefix(own_part, joiner, shifter):
    window_span = min(REACH_MAX, lax.axis_size("seq") // 2)
    levels = (window_span - 1).bit_length()
    gathered = shifter(own_part, 1)
    for degree in range(levels):
        received = shifter(gathered, 1 << degree)
        gathered = joiner(received, gathered)
    return gathered


def per_device(query_rows, key_rows, value_rows, log_gate, episode, grad_out):
    head_count, tokens, head_width = query_rows.shape
    stretch_count = tokens // STRETCH

    def partition_sets(values):
        return values.reshape(head_count, stretch_count, STRETCH, head_width)

    queries = partition_sets(query_rows)
    keyset = partition_sets(key_rows)
    values = partition_sets(value_rows)
    cotangent = partition_sets(grad_out)
    running = jnp.cumsum(log_gate.reshape(head_count, stretch_count, STRETCH), axis=-1)
    episodes = episode.reshape(stretch_count, STRETCH)
    causal = jnp.arange(STRETCH)[:, None] >= jnp.arange(STRETCH)[None, :]
    allowed = ((episodes[:, :, None] == episodes[:, None, :]) & causal[None])[None]
    differences = running[..., :, None] - running[..., None, :]
    decays = jnp.where(allowed, jnp.exp(jnp.where(allowed, differences, 0.0)), 0.0)
    scores = (
        jnp.einsum("hncd,hnsd->hncs", queries, keyset, preferred_element_type=jnp.float32) * decays
    ).astype(jnp.bfloat16)
    within = jnp.einsum("hncs,hnse->hnce", scores, values, preferred_element_type=jnp.float32)
    totals = running[..., -1]
    last_ids = episodes[:, -1]
    weight = jnp.where(
        (episodes == last_ids[:, None])[None], jnp.exp(running[..., -1:] - running), 0.0
    )
    keys_decayed = (keyset * weight[..., None]).astype(jnp.bfloat16)
    local_states = jnp.einsum(
        "hncd,hnce->hnde", keys_decayed, values, preferred_element_type=jnp.float32
    )
    stretch_parts = (totals[:, 0], local_states[:, 0], last_ids[0])
    incoming = window_prefix(stretch_parts, forward_join, shift_forward)
    entering = [incoming]
    state_low = jnp.stack([member[1] for member in entering], axis=1).astype(jnp.bfloat16)
    prior_ids = jnp.stack([member[2] for member in entering])
    carried = jnp.where((episodes == prior_ids[:, None])[None], jnp.exp(running), 0.0)
    attention = (
        within
        + jnp.einsum("hncd,hnde->hnce", queries, state_low, preferred_element_type=jnp.float32)
        * carried[..., None]
    )
    cotangent_wide = cotangent.astype(jnp.float32)
    squared_terms = jnp.sum(attention * attention, axis=(0, 3))
    crossed = jnp.sum(cotangent_wide * attention, axis=(0, 3))
    squared_terms, crossed = in_one((squared_terms, crossed), "head")
    features = head_count * lax.axis_size("head") * head_width
    root_mean = jnp.sqrt(squared_terms / features + EPSILON)
    normed = (attention / root_mean[None, :, :, None]).astype(jnp.bfloat16)
    grad_attn = (
        (
            cotangent_wide
            - attention * (crossed / (features * root_mean * root_mean))[None, :, :, None]
        )
        / root_mean[None, :, :, None]
    ).astype(jnp.bfloat16)
    score_gradient = (
        jnp.einsum("hnce,hnse->hncs", grad_attn, values, preferred_element_type=jnp.float32)
        * decays
    ).astype(jnp.bfloat16)
    first_ids = episodes[:, 0]
    query_weight = jnp.where((episodes == first_ids[:, None])[None], jnp.exp(running), 0.0)
    queries_decayed = (queries * query_weight[..., None]).astype(jnp.bfloat16)
    back_local = jnp.einsum(
        "hncd,hnce->hnde", queries_decayed, grad_attn, preferred_element_type=jnp.float32
    )
    back_parts = [(totals[:, 0], back_local[:, 0], first_ids[0])]
    back_summary = back_parts[stretch_count - 1]
    arriving = window_prefix(back_summary, reverse_merge_pass, shift_backward)
    query_grad = (
        jnp.einsum("hncs,hnsd->hncd", score_gradient, keyset, preferred_element_type=jnp.float32)
        + jnp.einsum("hnce,hnde->hncd", grad_attn, state_low, preferred_element_type=jnp.float32)
        * carried[..., None]
    )
    key_inner = jnp.einsum(
        "hncs,hncd->hnsd", score_gradient, queries, preferred_element_type=jnp.float32
    )
    value_inner = jnp.einsum(
        "hncs,hnce->hnse", scores, grad_attn, preferred_element_type=jnp.float32
    )
    leaving = [arriving]
    back_low = jnp.stack([member[1] for member in leaving], axis=1).astype(jnp.bfloat16)
    next_ids = jnp.stack([member[2] for member in leaving])
    trailing = jnp.where(
        (episodes == next_ids[:, None])[None], jnp.exp(running[..., -1:] - running), 0.0
    )
    key_grad = (
        key_inner
        + jnp.einsum("hnce,hnde->hncd", values, back_low, preferred_element_type=jnp.float32)
        * trailing[..., None]
    )
    value_grad = (
        value_inner
        + jnp.einsum("hncd,hnde->hnce", keyset, back_low, preferred_element_type=jnp.float32)
        * trailing[..., None]
    )

    def unblock(values_in):
        return values_in.reshape(head_count, tokens, head_width).astype(jnp.bfloat16)

    return (unblock(normed), unblock(query_grad), unblock(key_grad), unblock(value_grad))


def solution(mesh):
    placed = (
        P("head", "seq", None),
        P("head", "seq", None),
        P("head", "seq", None),
        P("head", "seq"),
        P("seq"),
        P("head", "seq", None),
    )
    return jax.shard_map(
        per_device,
        mesh=mesh,
        in_specs=placed,
        out_specs=(
            P("head", "seq", None),
            P("head", "seq", None),
            P("head", "seq", None),
            P("head", "seq", None),
        ),
        check_vma=False,
    )
```

profile of v0, /device:TPU:200, one launch (start us, length us, event | category | flops | bytes accessed | tf_op | source)
XLA Modules:
  0.0 234.7 jit_solution(15832060813186165904)
XLA Ops:
  0.7 0.7 copy-done.4
  1.4 0.6 fusion.28
  2.0 3.6 %collective-permute-start = (s32[]{:T(128)}, s32[]{:T(128)}, u32[]{:S(2)}, u32[]{:S(2)}) collective-permute-start(s32[]{:T(128)} %bitcast.5), channel_id=1, source_target_pairs={{0,8},{8,16},{16,24},{24,32},{32,40},{40,48},{48,56},{56,64},{64,7... | collective-permute-start | bytes 20 | tf_op jit(solution)/shard_map/ppermute | solution.py:16
  5.6 2.4 %collective-permute-start.14 = (s32[]{:T(128)}, s32[]{:T(128)}, u32[]{:S(2)}, u32[]{:S(2)}) collective-permute-start(s32[]{:T(128)} %bitcast.10), channel_id=1, source_target_pairs={{8,0},{16,8},{24,16},{32,24},{40,32},{48,40},{56,48},{64,56},{72,6... | collective-permute-start | bytes 20 | tf_op jit(solution)/shard_map/ppermute | solution.py:16
  8.0 1.2 reduce-window.6
  9.3 0.1 copy.82
  9.7 3.5 %collective-permute-start.1 = (s32[]{:T(128)}, s32[]{:T(128)}, u32[]{:S(2)}, u32[]{:S(2)}) collective-permute-start(s32[]{:T(128)} %collective-permute-done), channel_id=1, source_target_pairs={{0,8},{8,16},{16,24},{24,32},{32,40},{40,48},{48,56},{56,64},{64,7... | collective-permute-start | bytes 20 | tf_op jit(solution)/shard_map/ppermute | solution.py:16
  14.5 2.9 %collective-permute-start.15 = (s32[]{:T(128)}, s32[]{:T(128)}, u32[]{:S(2)}, u32[]{:S(2)}) collective-permute-start(s32[]{:T(128)} %collective-permute-done.14), channel_id=1, source_target_pairs={{8,0},{16,8},{24,16},{32,24},{40,32},{48,40},{56,48},{64,56},{72,6... | collective-permute-start | bytes 20 | tf_op jit(solution)/shard_map/ppermute | solution.py:16
  18.7 7.2 %collective-permute-start.2 = (s32[]{:T(128)}, s32[]{:T(128)}, u32[]{:S(2)}, u32[]{:S(2)}) collective-permute-start(s32[]{:T(128)} %select_n.173), channel_id=1, source_target_pairs={{0,16},{8,24},{16,32},{24,40},{32,48},{40,56},{48,64},{56,72},{64,... | collective-permute-start | bytes 20 | tf_op jit(solution)/shard_map/ppermute | solution.py:16
  27.2 4.2 %collective-permute-start.16 = (s32[]{:T(128)}, s32[]{:T(128)}, u32[]{:S(2)}, u32[]{:S(2)}) collective-permute-start(s32[]{:T(128)} %select_n.195), channel_id=1, source_target_pairs={{16,0},{24,8},{32,16},{40,24},{48,32},{56,40},{64,48},{72,56},{80,... | collective-permute-start | bytes 20 | tf_op jit(solution)/shard_map/ppermute | solution.py:16
  32.1 7.4 %collective-permute-start.3 = (s32[]{:T(128)}, s32[]{:T(128)}, u32[]{:S(2)}, u32[]{:S(2)}) collective-permute-start(s32[]{:T(128)} %select_n.174), channel_id=1, source_target_pairs={{0,32},{8,40},{16,48},{24,56},{32,64},{40,72},{48,80},{56,88},{64,... | collective-permute-start | bytes 20 | tf_op jit(solution)/shard_map/ppermute | solution.py:16
  40.1 5.8 %collective-permute-start.17 = (s32[]{:T(128)}, s32[]{:T(128)}, u32[]{:S(2)}, u32[]{:S(2)}) collective-permute-start(s32[]{:T(128)} %select_n.196), channel_id=1, source_target_pairs={{32,0},{40,8},{48,16},{56,24},{64,32},{72,40},{80,48},{88,56},{96,... | collective-permute-start | bytes 20 | tf_op jit(solution)/shard_map/ppermute | solution.py:16
  46.6 11.3 %collective-permute-start.12 = (s32[]{:T(128)}, s32[]{:T(128)}, u32[]{:S(2)}, u32[]{:S(2)}) collective-permute-start(s32[]{:T(128)} %select_n.175), channel_id=1, source_target_pairs={{0,64},{8,72},{16,80},{24,88},{32,96},{40,104},{48,112},{56,120},{... | collective-permute-start | bytes 20 | tf_op jit(solution)/shard_map/ppermute | solution.py:16
  58.4 3.2 %collective-permute-start.26 = (s32[]{:T(128)}, s32[]{:T(128)}, u32[]{:S(2)}, u32[]{:S(2)}) collective-permute-start(s32[]{:T(128)} %select_n.197), channel_id=1, source_target_pairs={{64,0},{72,8},{80,16},{88,24},{96,32},{104,40},{112,48},{120,56},{... | collective-permute-start | bytes 20 | tf_op jit(solution)/shard_map/ppermute | solution.py:16
  62.3 2.9 %collective-permute-done.26 = s32[]{:T(128)} collective-permute-done((s32[]{:T(128)}, s32[]{:T(128)}, u32[]{:S(2)}, u32[]{:S(2)}) %collective-permute-start.26) | collective-permute-done | bytes 36 | tf_op jit(solution)/shard_map/ppermute | solution.py:16
  65.8 1.3 broadcast_compare_fusion.1
  67.3 0.5 fusion.15
  67.8 1.9 collective-permute-start.4
  69.7 9.9 %collective-permute-done.4 = f32[4,128,128]{2,1,0:T(8,128)S(1)} collective-permute-done((f32[4,128,128]{2,1,0:T(8,128)S(1)}, f32[4,128,128]{2,1,0:T(8,128)S(1)}, u32[]{:S(2)}, u32[]{:S(2)}) %collective-permute-start.4) | collective-permute-done | bytes 262176 | tf_op jit(solution)/shard_map/ppermute | solution.py:16
  79.6 1.9 collective-permute-start.5
  81.5 3.7 %collective-permute-start.6 = (f32[4]{0:T(128)S(1)}, f32[4]{0:T(128)S(1)}, u32[]{:S(2)}, u32[]{:S(2)}) collective-permute-start(f32[4]{0:T(128)S(1)} %fusion.23), channel_id=1, source_target_pairs={{0,8},{8,16},{16,24},{24,32},{32,40},{40,48},{48,56},{56,64},{64,7... | collective-permute-start | bytes 56 | tf_op jit(solution)/shard_map/ppermute | solution.py:16
  86.5 3.8 %collective-permute-done.6 = f32[4]{0:T(128)S(1)} collective-permute-done((f32[4]{0:T(128)S(1)}, f32[4]{0:T(128)S(1)}, u32[]{:S(2)}, u32[]{:S(2)}) %collective-permute-start.6) | collective-permute-done | bytes 48 | tf_op jit(solution)/shard_map/ppermute | solution.py:16
  90.3 1.9 collective-permute-start.8
  92.2 6.5 %collective-permute-done.8 = f32[4]{0:T(128)S(1)} collective-permute-done((f32[4]{0:T(128)S(1)}, f32[4]{0:T(128)S(1)}, u32[]{:S(2)}, u32[]{:S(2)}) %collective-permute-start.8) | collective-permute-done | bytes 48 | tf_op jit(solution)/shard_map/ppermute | solution.py:16
  98.8 1.9 collective-permute-start.7
  100.8 0.1 copy.55
  102.3 9.6 %collective-permute-done.7 = f32[4,128,128]{2,1,0:T(8,128)S(1)} collective-permute-done((f32[4,128,128]{2,1,0:T(8,128)S(1)}, f32[4,128,128]{2,1,0:T(8,128)S(1)}, u32[]{:S(2)}, u32[]{:S(2)}) %collective-permute-start.7) | collective-permute-done | bytes 262176 | tf_op jit(solution)/shard_map/ppermute | solution.py:16
  112.0 8.1 %collective-permute-start.9 = (f32[4,128,128]{2,1,0:T(8,128)S(1)}, f32[4,128,128]{2,1,0:T(8,128)S(1)}, u32[]{:S(2)}, u32[]{:S(2)}) collective-permute-start(f32[4,128,128]{2,1,0:T(8,128)S(1)} %add_select_fusion.4), channel_id=1, source_target_pairs={{0,32},{8,40},{16,48},{24,56},{32,64},{40,72},{48,80},{56,88},{64,... | collective-permute-start | bytes 786440 | tf_op jit(solution)/shard_map/ppermute | solution.py:16
  120.1 0.4 fusion
  120.5 6.1 %collective-permute-start.10 = (f32[4]{0:T(128)S(1)}, f32[4]{0:T(128)S(1)}, u32[]{:S(2)}, u32[]{:S(2)}) collective-permute-start(f32[4]{0:T(128)S(1)} %get-tuple-element.27), channel_id=1, source_target_pairs={{0,16},{8,24},{16,32},{24,40},{32,48},{40,56},{48,64},{56,72},{64,... | collective-permute-start | bytes 56 | tf_op jit(solution)/shard_map/ppermute | solution.py:16
  126.6 2.3 collective-permute-done.10
  129.1 3.1 %collective-permute-start.11 = (f32[4,128,128]{2,1,0:T(8,128)S(1)}, f32[4,128,128]{2,1,0:T(8,128)S(1)}, u32[]{:S(2)}, u32[]{:S(2)}) collective-permute-start(f32[4,128,128]{2,1,0:T(8,128)S(1)} %add_select_fusion.3), channel_id=1, source_target_pairs={{0,64},{8,72},{16,80},{24,88},{32,96},{40,104},{48,112},{56,120},{... | collective-permute-start | bytes 786440 | tf_op jit(solution)/shard_map/ppermute | solution.py:16
  132.2 0.3 fusion.29
  133.2 3.7 %collective-permute-start.13 = (f32[4]{0:T(128)S(1)}, f32[4]{0:T(128)S(1)}, u32[]{:S(2)}, u32[]{:S(2)}) collective-permute-start(f32[4]{0:T(128)S(1)} %get-tuple-element.25), channel_id=1, source_target_pairs={{0,32},{8,40},{16,48},{24,56},{32,64},{40,72},{48,80},{56,88},{64,... | collective-permute-start | bytes 56 | tf_op jit(solution)/shard_map/ppermute | solution.py:16
  136.9 6.5 %collective-permute-done.13 = f32[4]{0:T(128)S(1)} collective-permute-done((f32[4]{0:T(128)S(1)}, f32[4]{0:T(128)S(1)}, u32[]{:S(2)}, u32[]{:S(2)}) %collective-permute-start.13) | collective-permute-done | bytes 48 | tf_op jit(solution)/shard_map/ppermute | solution.py:16
  143.5 0.1 select_convert_fusion.1
  143.6 0.3 multiply_reduce_fusion
  144.0 9.5 %all_to_all.6 = f32[8,1,512]{2,1,0:T(1,128)S(1)} all-to-all(f32[8,1,512]{2,1,0:T(1,128)S(1)} %broadcast_in_dim.93), channel_id=1, replica_groups=mesh['seq'=128,'head'=8] {'head'}, dimensions={0} | all-to-all | bytes 32768 | tf_op jit(solution)/shard_map/all_to_all | solution.py:21
  153.5 0.1 fusion.14
  153.6 0.5 fusion.16
  154.1 8.4 %collective-permute-start.18 = (f32[4,128,128]{2,1,0:T(8,128)S(1)}, f32[4,128,128]{2,1,0:T(8,128)S(1)}, u32[]{:S(2)}, u32[]{:S(2)}) collective-permute-start(f32[4,128,128]{2,1,0:T(8,128)S(1)} %fusion.16), channel_id=1, source_target_pairs={{8,0},{16,8},{24,16},{32,24},{40,32},{48,40},{56,48},{64,56},{72,6... | collective-permute-start | bytes 786440 | tf_op jit(solution)/shard_map/ppermute | solution.py:16
  162.5 1.9 collective-permute-start.20
  167.0 1.1 collective-permute-done.20
  168.1 4.4 %collective-permute-start.22 = (f32[4]{0:T(128)S(1)}, f32[4]{0:T(128)S(1)}, u32[]{:S(2)}, u32[]{:S(2)}) collective-permute-start(f32[4]{0:T(128)S(1)} %collective-permute-done.20), channel_id=1, source_target_pairs={{8,0},{16,8},{24,16},{32,24},{40,32},{48,40},{56,48},{64,56},{72,6... | collective-permute-start | bytes 56 | tf_op jit(solution)/shard_map/ppermute | solution.py:16
  173.1 4.3 %collective-permute-start.19 = (f32[4,128,128]{2,1,0:T(8,128)S(1)}, f32[4,128,128]{2,1,0:T(8,128)S(1)}, u32[]{:S(2)}, u32[]{:S(2)}) collective-permute-start(f32[4,128,128]{2,1,0:T(8,128)S(1)} %collective-permute-done.18), channel_id=1, source_target_pairs={{8,0},{16,8},{24,16},{32,24},{40,32},{48,40},{56,48},{64,56},{72,6... | collective-permute-start | bytes 786440 | tf_op jit(solution)/shard_map/ppermute | solution.py:16
  177.5 4.5 %collective-permute-start.24 = (f32[4]{0:T(128)S(1)}, f32[4]{0:T(128)S(1)}, u32[]{:S(2)}, u32[]{:S(2)}) collective-permute-start(f32[4]{0:T(128)S(1)} %get-tuple-element.23), channel_id=1, source_target_pairs={{16,0},{24,8},{32,16},{40,24},{48,32},{56,40},{64,48},{72,56},{80,... | collective-permute-start | bytes 56 | tf_op jit(solution)/shard_map/ppermute | solution.py:16
  181.9 1.9 collective-permute-done.24
  183.8 3.9 %collective-permute-start.27 = (f32[4]{0:T(128)S(1)}, f32[4]{0:T(128)S(1)}, u32[]{:S(2)}, u32[]{:S(2)}) collective-permute-start(f32[4]{0:T(128)S(1)} %get-tuple-element.21), channel_id=1, source_target_pairs={{32,0},{40,8},{48,16},{56,24},{64,32},{72,40},{80,48},{88,56},{96,... | collective-permute-start | bytes 56 | tf_op jit(solution)/shard_map/ppermute | solution.py:16
  187.9 4.6 %collective-permute-start.21 = (f32[4,128,128]{2,1,0:T(8,128)S(1)}, f32[4,128,128]{2,1,0:T(8,128)S(1)}, u32[]{:S(2)}, u32[]{:S(2)}) collective-permute-start(f32[4,128,128]{2,1,0:T(8,128)S(1)} %add_select_fusion.2), channel_id=1, source_target_pairs={{16,0},{24,8},{32,16},{40,24},{48,32},{56,40},{64,48},{72,56},{80,... | collective-permute-start | bytes 786440 | tf_op jit(solution)/shard_map/ppermute | solution.py:16
  192.5 0.8 collective-permute-done.27
  193.3 0.3 fusion.32
  193.7 9.1 %collective-permute-done.21 = f32[4,128,128]{2,1,0:T(8,128)S(1)} collective-permute-done((f32[4,128,128]{2,1,0:T(8,128)S(1)}, f32[4,128,128]{2,1,0:T(8,128)S(1)}, u32[]{:S(2)}, u32[]{:S(2)}) %collective-permute-start.21) | collective-permute-done | bytes 262176 | tf_op jit(solution)/shard_map/ppermute | solution.py:16
  202.9 3.5 %collective-permute-start.23 = (f32[4,128,128]{2,1,0:T(8,128)S(1)}, f32[4,128,128]{2,1,0:T(8,128)S(1)}, u32[]{:S(2)}, u32[]{:S(2)}) collective-permute-start(f32[4,128,128]{2,1,0:T(8,128)S(1)} %add_select_fusion.1), channel_id=1, source_target_pairs={{32,0},{40,8},{48,16},{56,24},{64,32},{72,40},{80,48},{88,56},{96,... | collective-permute-start | bytes 786440 | tf_op jit(solution)/shard_map/ppermute | solution.py:16
  206.3 0.5 fusion.1
  206.8 0.3 fusion.30
  207.1 13.9 %collective-permute-done.23 = f32[4,128,128]{2,1,0:T(8,128)S(1)} collective-permute-done((f32[4,128,128]{2,1,0:T(8,128)S(1)}, f32[4,128,128]{2,1,0:T(8,128)S(1)}, u32[]{:S(2)}, u32[]{:S(2)}) %collective-permute-start.23) | collective-permute-done | bytes 262176 | tf_op jit(solution)/shard_map/ppermute | solution.py:16
  221.2 1.9 collective-permute-start.25
  223.1 1.0 fusion.9
  224.1 0.8 copy.67
  225.0 0.3 fusion.31
  225.3 7.4 %collective-permute-done.25 = f32[4,128,128]{2,1,0:T(8,128)S(1)} collective-permute-done((f32[4,128,128]{2,1,0:T(8,128)S(1)}, f32[4,128,128]{2,1,0:T(8,128)S(1)}, u32[]{:S(2)}, u32[]{:S(2)}) %collective-permute-start.25) | collective-permute-done | bytes 262176 | tf_op jit(solution)/shard_map/ppermute | solution.py:16
  232.7 0.1 select_convert_fusion
  232.8 0.9 fusion.11
  233.7 0.9 fusion.10
  (53 shorter events, 1.4 us)
Async XLA Ops:
  0.6 66.6 %copy-start = (bf16[4,256,128]{2,1,0:T(8,128)(2,1)S(1)}, bf16[4,256,128]{2,1,0:T(8,128)(2,1)}, u32[]{:S(2)}) copy-start(bf16[4,256,128]{2,1,0:T(8,128)(2,1)} %param.8) | copy-start | bytes 786436
  0.6 0.7 copy-start.4
  2.0 6.0 %copy-start.5 = (f32[4,256]{1,0:T(4,128)S(1)}, f32[4,256]{1,0:T(4,128)}, u32[]{:S(2)}) copy-start(f32[4,256]{1,0:T(4,128)} %param.9) | copy-start | bytes 12292
  2.0 7.7 %collective-permute-start = (s32[]{:T(128)}, s32[]{:T(128)}, u32[]{:S(2)}, u32[]{:S(2)}) collective-permute-start(s32[]{:T(128)} %bitcast.5), channel_id=1, source_target_pairs={{0,8},{8,16},{16,24},{24,32},{32,40},{40,48},{48,56},{56,64},{64,7... | collective-permute-start | bytes 20 | tf_op jit(solution)/shard_map/ppermute | solution.py:16
  5.6 8.3 %collective-permute-start.14 = (s32[]{:T(128)}, s32[]{:T(128)}, u32[]{:S(2)}, u32[]{:S(2)}) collective-permute-start(s32[]{:T(128)} %bitcast.10), channel_id=1, source_target_pairs={{8,0},{16,8},{24,16},{32,24},{40,32},{48,40},{56,48},{64,56},{72,6... | collective-permute-start | bytes 20 | tf_op jit(solution)/shard_map/ppermute | solution.py:16
  8.0 59.3 %copy-start.2 = (bf16[4,256,128]{2,1,0:T(8,128)(2,1)S(1)}, bf16[4,256,128]{2,1,0:T(8,128)(2,1)}, u32[]{:S(2)}) copy-start(bf16[4,256,128]{2,1,0:T(8,128)(2,1)} %param.7) | copy-start | bytes 786436
  9.7 7.7 %collective-permute-start.1 = (s32[]{:T(128)}, s32[]{:T(128)}, u32[]{:S(2)}, u32[]{:S(2)}) collective-permute-start(s32[]{:T(128)} %collective-permute-done), channel_id=1, source_target_pairs={{0,8},{8,16},{16,24},{24,32},{32,40},{40,48},{48,56},{56,64},{64,7... | collective-permute-start | bytes 20 | tf_op jit(solution)/shard_map/ppermute | solution.py:16
  14.5 11.4 %collective-permute-start.15 = (s32[]{:T(128)}, s32[]{:T(128)}, u32[]{:S(2)}, u32[]{:S(2)}) collective-permute-start(s32[]{:T(128)} %collective-permute-done.14), channel_id=1, source_target_pairs={{8,0},{16,8},{24,16},{32,24},{40,32},{48,40},{56,48},{64,56},{72,6... | collective-permute-start | bytes 20 | tf_op jit(solution)/shard_map/ppermute | solution.py:16
  18.7 12.7 %collective-permute-start.2 = (s32[]{:T(128)}, s32[]{:T(128)}, u32[]{:S(2)}, u32[]{:S(2)}) collective-permute-start(s32[]{:T(128)} %select_n.173), channel_id=1, source_target_pairs={{0,16},{8,24},{16,32},{24,40},{32,48},{40,56},{48,64},{56,72},{64,... | collective-permute-start | bytes 20 | tf_op jit(solution)/shard_map/ppermute | solution.py:16
  27.2 12.3 %collective-permute-start.16 = (s32[]{:T(128)}, s32[]{:T(128)}, u32[]{:S(2)}, u32[]{:S(2)}) collective-permute-start(s32[]{:T(128)} %select_n.195), channel_id=1, source_target_pairs={{16,0},{24,8},{32,16},{40,24},{48,32},{56,40},{64,48},{72,56},{80,... | collective-permute-start | bytes 20 | tf_op jit(solution)/shard_map/ppermute | solution.py:16
  32.1 13.9 %collective-permute-start.3 = (s32[]{:T(128)}, s32[]{:T(128)}, u32[]{:S(2)}, u32[]{:S(2)}) collective-permute-start(s32[]{:T(128)} %select_n.174), channel_id=1, source_target_pairs={{0,32},{8,40},{16,48},{24,56},{32,64},{40,72},{48,80},{56,88},{64,... | collective-permute-start | bytes 20 | tf_op jit(solution)/shard_map/ppermute | solution.py:16
  40.1 17.7 %collective-permute-start.17 = (s32[]{:T(128)}, s32[]{:T(128)}, u32[]{:S(2)}, u32[]{:S(2)}) collective-permute-start(s32[]{:T(128)} %select_n.196), channel_id=1, source_target_pairs={{32,0},{40,8},{48,16},{56,24},{64,32},{72,40},{80,48},{88,56},{96,... | collective-permute-start | bytes 20 | tf_op jit(solution)/shard_map/ppermute | solution.py:16
  46.6 15.1 %collective-permute-start.12 = (s32[]{:T(128)}, s32[]{:T(128)}, u32[]{:S(2)}, u32[]{:S(2)}) collective-permute-start(s32[]{:T(128)} %select_n.175), channel_id=1, source_target_pairs={{0,64},{8,72},{16,80},{24,88},{32,96},{40,104},{48,112},{56,120},{... | collective-permute-start | bytes 20 | tf_op jit(solution)/shard_map/ppermute | solution.py:16
  58.4 6.8 %collective-permute-start.26 = (s32[]{:T(128)}, s32[]{:T(128)}, u32[]{:S(2)}, u32[]{:S(2)}) collective-permute-start(s32[]{:T(128)} %select_n.197), channel_id=1, source_target_pairs={{64,0},{72,8},{80,16},{88,24},{96,32},{104,40},{112,48},{120,56},{... | collective-permute-start | bytes 20 | tf_op jit(solution)/shard_map/ppermute | solution.py:16
  67.8 11.8 %collective-permute-start.4 = (f32[4,128,128]{2,1,0:T(8,128)S(1)}, f32[4,128,128]{2,1,0:T(8,128)S(1)}, u32[]{:S(2)}, u32[]{:S(2)}) collective-permute-start(f32[4,128,128]{2,1,0:T(8,128)S(1)} %fusion.15), channel_id=1, source_target_pairs={{0,8},{8,16},{16,24},{24,32},{32,40},{40,48},{48,56},{56,64},{64,7... | collective-permute-start | bytes 786440 | tf_op jit(solution)/shard_map/ppermute | solution.py:16
  79.6 19.1 %collective-permute-start.5 = (f32[4,128,128]{2,1,0:T(8,128)S(1)}, f32[4,128,128]{2,1,0:T(8,128)S(1)}, u32[]{:S(2)}, u32[]{:S(2)}) collective-permute-start(f32[4,128,128]{2,1,0:T(8,128)S(1)} %collective-permute-done.4), channel_id=1, source_target_pairs={{0,8},{8,16},{16,24},{24,32},{32,40},{40,48},{48,56},{56,64},{64,7... | collective-permute-start | bytes 786440 | tf_op jit(solution)/shard_map/ppermute | solution.py:16
  81.5 8.8 %collective-permute-start.6 = (f32[4]{0:T(128)S(1)}, f32[4]{0:T(128)S(1)}, u32[]{:S(2)}, u32[]{:S(2)}) collective-permute-start(f32[4]{0:T(128)S(1)} %fusion.23), channel_id=1, source_target_pairs={{0,8},{8,16},{16,24},{24,32},{32,40},{40,48},{48,56},{56,64},{64,7... | collective-permute-start | bytes 56 | tf_op jit(solution)/shard_map/ppermute | solution.py:16
  90.3 8.4 %collective-permute-start.8 = (f32[4]{0:T(128)S(1)}, f32[4]{0:T(128)S(1)}, u32[]{:S(2)}, u32[]{:S(2)}) collective-permute-start(f32[4]{0:T(128)S(1)} %collective-permute-done.6), channel_id=1, source_target_pairs={{0,8},{8,16},{16,24},{24,32},{32,40},{40,48},{48,56},{56,64},{64,7... | collective-permute-start | bytes 56 | tf_op jit(solution)/shard_map/ppermute | solution.py:16
  98.7 2.1 copy-start.3
  98.8 13.0 %collective-permute-start.7 = (f32[4,128,128]{2,1,0:T(8,128)S(1)}, f32[4,128,128]{2,1,0:T(8,128)S(1)}, u32[]{:S(2)}, u32[]{:S(2)}) collective-permute-start(f32[4,128,128]{2,1,0:T(8,128)S(1)} %add_select_fusion.5), channel_id=1, source_target_pairs={{0,16},{8,24},{16,32},{24,40},{32,48},{40,56},{48,64},{56,72},{64,... | collective-permute-start | bytes 786440 | tf_op jit(solution)/shard_map/ppermute | solution.py:16
  111.9 8.2 %copy-start.1 = (bf16[4,256,128]{2,1,0:T(8,128)(2,1)S(1)}, bf16[4,256,128]{2,1,0:T(8,128)(2,1)}, u32[]{:S(2)}) copy-start(bf16[4,256,128]{2,1,0:T(8,128)(2,1)} %param.6) | copy-start | bytes 786436
  112.0 17.0 %collective-permute-start.9 = (f32[4,128,128]{2,1,0:T(8,128)S(1)}, f32[4,128,128]{2,1,0:T(8,128)S(1)}, u32[]{:S(2)}, u32[]{:S(2)}) collective-permute-start(f32[4,128,128]{2,1,0:T(8,128)S(1)} %add_select_fusion.4), channel_id=1, source_target_pairs={{0,32},{8,40},{16,48},{24,56},{32,64},{40,72},{48,80},{56,88},{64,... | collective-permute-start | bytes 786440 | tf_op jit(solution)/shard_map/ppermute | solution.py:16
  120.5 8.5 %collective-permute-start.10 = (f32[4]{0:T(128)S(1)}, f32[4]{0:T(128)S(1)}, u32[]{:S(2)}, u32[]{:S(2)}) collective-permute-start(f32[4]{0:T(128)S(1)} %get-tuple-element.27), channel_id=1, source_target_pairs={{0,16},{8,24},{16,32},{24,40},{32,48},{40,56},{48,64},{56,72},{64,... | collective-permute-start | bytes 56 | tf_op jit(solution)/shard_map/ppermute | solution.py:16
  129.1 14.4 %collective-permute-start.11 = (f32[4,128,128]{2,1,0:T(8,128)S(1)}, f32[4,128,128]{2,1,0:T(8,128)S(1)}, u32[]{:S(2)}, u32[]{:S(2)}) collective-permute-start(f32[4,128,128]{2,1,0:T(8,128)S(1)} %add_select_fusion.3), channel_id=1, source_target_pairs={{0,64},{8,72},{16,80},{24,88},{32,96},{40,104},{48,112},{56,120},{... | collective-permute-start | bytes 786440 | tf_op jit(solution)/shard_map/ppermute | solution.py:16
  133.2 10.3 %collective-permute-start.13 = (f32[4]{0:T(128)S(1)}, f32[4]{0:T(128)S(1)}, u32[]{:S(2)}, u32[]{:S(2)}) collective-permute-start(f32[4]{0:T(128)S(1)} %get-tuple-element.25), channel_id=1, source_target_pairs={{0,32},{8,40},{16,48},{24,56},{32,64},{40,72},{48,80},{56,88},{64,... | collective-permute-start | bytes 56 | tf_op jit(solution)/shard_map/ppermute | solution.py:16
  154.1 19.0 %collective-permute-start.18 = (f32[4,128,128]{2,1,0:T(8,128)S(1)}, f32[4,128,128]{2,1,0:T(8,128)S(1)}, u32[]{:S(2)}, u32[]{:S(2)}) collective-permute-start(f32[4,128,128]{2,1,0:T(8,128)S(1)} %fusion.16), channel_id=1, source_target_pairs={{8,0},{16,8},{24,16},{32,24},{40,32},{48,40},{56,48},{64,56},{72,6... | collective-permute-start | bytes 786440 | tf_op jit(solution)/shard_map/ppermute | solution.py:16
  162.5 5.6 %collective-permute-start.20 = (f32[4]{0:T(128)S(1)}, f32[4]{0:T(128)S(1)}, u32[]{:S(2)}, u32[]{:S(2)}) collective-permute-start(f32[4]{0:T(128)S(1)} %fusion.23), channel_id=1, source_target_pairs={{8,0},{16,8},{24,16},{32,24},{40,32},{48,40},{56,48},{64,56},{72,6... | collective-permute-start | bytes 56 | tf_op jit(solution)/shard_map/ppermute | solution.py:16
  168.1 9.3 %collective-permute-start.22 = (f32[4]{0:T(128)S(1)}, f32[4]{0:T(128)S(1)}, u32[]{:S(2)}, u32[]{:S(2)}) collective-permute-start(f32[4]{0:T(128)S(1)} %collective-permute-done.20), channel_id=1, source_target_pairs={{8,0},{16,8},{24,16},{32,24},{40,32},{48,40},{56,48},{64,56},{72,6... | collective-permute-start | bytes 56 | tf_op jit(solution)/shard_map/ppermute | solution.py:16
  173.1 14.6 %collective-permute-start.19 = (f32[4,128,128]{2,1,0:T(8,128)S(1)}, f32[4,128,128]{2,1,0:T(8,128)S(1)}, u32[]{:S(2)}, u32[]{:S(2)}) collective-permute-start(f32[4,128,128]{2,1,0:T(8,128)S(1)} %collective-permute-done.18), channel_id=1, source_target_pairs={{8,0},{16,8},{24,16},{32,24},{40,32},{48,40},{56,48},{64,56},{72,6... | collective-permute-start | bytes 786440 | tf_op jit(solution)/shard_map/ppermute | solution.py:16
  177.5 6.4 %collective-permute-start.24 = (f32[4]{0:T(128)S(1)}, f32[4]{0:T(128)S(1)}, u32[]{:S(2)}, u32[]{:S(2)}) collective-permute-start(f32[4]{0:T(128)S(1)} %get-tuple-element.23), channel_id=1, source_target_pairs={{16,0},{24,8},{32,16},{40,24},{48,32},{56,40},{64,48},{72,56},{80,... | collective-permute-start | bytes 56 | tf_op jit(solution)/shard_map/ppermute | solution.py:16
  183.8 9.5 %collective-permute-start.27 = (f32[4]{0:T(128)S(1)}, f32[4]{0:T(128)S(1)}, u32[]{:S(2)}, u32[]{:S(2)}) collective-permute-start(f32[4]{0:T(128)S(1)} %get-tuple-element.21), channel_id=1, source_target_pairs={{32,0},{40,8},{48,16},{56,24},{64,32},{72,40},{80,48},{88,56},{96,... | collective-permute-start | bytes 56 | tf_op jit(solution)/shard_map/ppermute | solution.py:16
  187.9 14.9 %collective-permute-start.21 = (f32[4,128,128]{2,1,0:T(8,128)S(1)}, f32[4,128,128]{2,1,0:T(8,128)S(1)}, u32[]{:S(2)}, u32[]{:S(2)}) collective-permute-start(f32[4,128,128]{2,1,0:T(8,128)S(1)} %add_select_fusion.2), channel_id=1, source_target_pairs={{16,0},{24,8},{32,16},{40,24},{48,32},{56,40},{64,48},{72,56},{80,... | collective-permute-start | bytes 786440 | tf_op jit(solution)/shard_map/ppermute | solution.py:16
  202.9 18.2 %collective-permute-start.23 = (f32[4,128,128]{2,1,0:T(8,128)S(1)}, f32[4,128,128]{2,1,0:T(8,128)S(1)}, u32[]{:S(2)}, u32[]{:S(2)}) collective-permute-start(f32[4,128,128]{2,1,0:T(8,128)S(1)} %add_select_fusion.1), channel_id=1, source_target_pairs={{32,0},{40,8},{48,16},{56,24},{64,32},{72,40},{80,48},{88,56},{96,... | collective-permute-start | bytes 786440 | tf_op jit(solution)/shard_map/ppermute | solution.py:16
  221.2 11.5 %collective-permute-start.25 = (f32[4,128,128]{2,1,0:T(8,128)S(1)}, f32[4,128,128]{2,1,0:T(8,128)S(1)}, u32[]{:S(2)}, u32[]{:S(2)}) collective-permute-start(f32[4,128,128]{2,1,0:T(8,128)S(1)} %add_select_fusion), channel_id=1, source_target_pairs={{64,0},{72,8},{80,16},{88,24},{96,32},{104,40},{112,48},{120,56},{... | collective-permute-start | bytes 786440 | tf_op jit(solution)/shard_map/ppermute | solution.py:16
where the time goes:
time: 236 us; the launch traced here: 235 us
  starting transfers between devices  121 us (51%)
  waiting for transfers between devices  75.8 us (32%)
  between operations  15 us (6%)
  blocking collectives  9.47 us (4%)
  matrix products  6.35 us (3%)
  other arithmetic  3.89 us (2%)
  local copies, waits for them, and re-layouts  2.74 us (1%)
    ppermute x28, starting transfers between devices, passed_along(): return lax.ppermute(block, axis, route)  121 us
    ppermute x28, waiting for transfers between devices, passed_along(): return lax.ppermute(block, axis, route)  75.8 us
    all_to_all x1, blocking collectives, from_everyone(): return lax.all_to_all(copies, axis, split_axis=0, concat_axis=0, tiled=True)  9.47 us
  transfers between devices with their start and end apart: 28, of which 13 were waited for; matrix products, arithmetic and copies ran while one was open for 3% of the time, Pallas kernels for 0%

commit v1 on v0

v1 whole, which is shorter than its diff:
```python
import functools

import jax
import jax.numpy as jnp
from jax import lax
from jax.experimental import pallas as pl
from jax.experimental.pallas import tpu as pltpu
from jax.sharding import PartitionSpec as P

EPSILON = 1e-06
ROW = 16
META = 8
HIGH = lax.Precision.HIGHEST


def dot(a, b, da, db):
    return lax.dot_general(
        a, b, (((da,), (db,)), ((), ())), preferred_element_type=jnp.float32
    )


def call(body, outs, flops, scratch=()):
    shapes = [jax.ShapeDtypeStruct(s, d) for s, d in outs]

    def run(*args):
        size = sum(a.size * a.dtype.itemsize for a in (*args, *shapes))
        return pl.pallas_call(
            body,
            out_shape=shapes,
            in_specs=[pl.BlockSpec(memory_space=pltpu.VMEM)] * len(args),
            out_specs=[pl.BlockSpec(memory_space=pltpu.VMEM)] * len(shapes),
            scratch_shapes=list(scratch),
            cost_estimate=pl.CostEstimate(flops=flops, bytes_accessed=size, transcendentals=0),
            compiler_params=pltpu.CompilerParams(vmem_limit_bytes=8 << 20),
            name=body.__name__ if hasattr(body, "__name__") else body.func.__name__,
        )(*args)

    return run


def local_states(gate_ref, ep_ref, k_ref, v_ref, pay_ref, rows_ref, cols_ref):
    heads, tokens = gate_ref.shape
    width = k_ref.shape[2]
    per_head = ROW // heads
    depth = width // per_head
    run = gate_ref[...]
    place = lax.broadcasted_iota(jnp.int32, run.shape, 1)
    step = 1
    while step < tokens:
        run = run + jnp.where(place >= step, pltpu.roll(run, step, 1), 0.0)
        step *= 2
    total = run[:, tokens - 1 :]
    ep = ep_ref[...]
    first, last = ep[:, :1], ep[:, tokens - 1 :]
    rows_ref[...] = jnp.zeros(rows_ref.shape, jnp.float32)
    rows_ref[0:heads] = run
    rows_ref[heads : 2 * heads] = jnp.where(ep == first, jnp.exp(run), 0.0)
    rows_ref[2 * heads : 3 * heads] = jnp.where(ep == last, jnp.exp(total - run), 0.0)
    rows_ref[3 * heads : 3 * heads + 1] = ep.astype(jnp.float32)
    cols_ref[...] = rows_ref[...].T
    fact = lax.broadcasted_iota(jnp.int32, (META, width), 0)
    first_f, last_f = first.astype(jnp.float32), last.astype(jnp.float32)
    for h in range(heads):
        leave = cols_ref[:, 2 * heads + h : 2 * heads + h + 1]
        decayed = (k_ref[h].astype(jnp.float32) * leave).astype(jnp.bfloat16)
        state = dot(decayed, v_ref[h], 0, 0)
        facts = jnp.where(
            fact == 0,
            total[h : h + 1],
            jnp.where(fact == 1, first_f, jnp.where(fact == 2, last_f, 0.0)),
        )
        for part in range(per_head):
            p = h * per_head + part
            pay_ref[p, 0:depth] = state[part * depth : (part + 1) * depth]
            pay_ref[p, depth : depth + META] = facts


def facts_of(fact_ref, j):
    return fact_ref[j, 0:1], fact_ref[j, 1:2], fact_ref[j, 2:3]


def summary(sum_ref, state, mark):
    depth = state.shape[0]
    row = lax.broadcasted_iota(jnp.int32, (META, state.shape[1]), 0)
    sum_ref[0:depth] = state
    sum_ref[depth : depth + META] = jnp.where(row == 1, mark, 0.0)


def forward_row(got_ref, sum_ref, fact_ref):
    depth = got_ref.shape[1] - META
    for j in range(ROW):
        fact_ref[j] = got_ref[j, depth : depth + META]
    state, mark = got_ref[0, 0:depth], facts_of(fact_ref, 0)[2]
    for j in range(1, ROW):
        decay, _, last = facts_of(fact_ref, j)
        state = jnp.where(mark == last, jnp.exp(decay), 0.0) * state + got_ref[j, 0:depth]
        mark = last
    summary(sum_ref, state, mark)


def backward_row(got_ref, fact_ref, sum_ref):
    state, mark = got_ref[ROW - 1], facts_of(fact_ref, ROW - 1)[1]
    for j in range(ROW - 2, -1, -1):
        decay, first, _ = facts_of(fact_ref, j)
        state = jnp.where(mark == first, jnp.exp(decay), 0.0) * state + got_ref[j]
        mark = first
    summary(sum_ref, state, mark)


def forward_scan(got_ref, fact_ref, near_ref, out_ref):
    depth = out_ref.shape[1]
    state, mark = near_ref[0:depth], near_ref[depth + 1 : depth + 2]
    for j in range(ROW):
        decay, first, last = facts_of(fact_ref, j)
        out_ref[j] = jnp.where(mark == first, state, 0.0)
        state = jnp.where(mark == last, jnp.exp(decay), 0.0) * state + got_ref[j, 0:depth]
        mark = last


def backward_scan(got_ref, fact_ref, near_ref, out_ref):
    depth = out_ref.shape[1]
    state, mark = near_ref[0:depth], near_ref[depth + 1 : depth + 2]
    for j in range(ROW - 1, -1, -1):
        decay, first, last = facts_of(fact_ref, j)
        out_ref[j] = jnp.where(mark == last, state, 0.0)
        state = jnp.where(mark == first, jnp.exp(decay), 0.0) * state + got_ref[j]
        mark = first


def decays_of(rows_ref, cols_ref, heads, h):
    tokens = cols_ref.shape[0]
    later = lax.broadcasted_iota(jnp.int32, (tokens, tokens), 0)
    earlier = lax.broadcasted_iota(jnp.int32, (tokens, tokens), 1)
    one = 3 * heads
    allowed = (cols_ref[:, one : one + 1] == rows_ref[one : one + 1]) & (later >= earlier)
    difference = cols_ref[:, h : h + 1] - rows_ref[h : h + 1]
    return jnp.where(allowed, jnp.exp(jnp.where(allowed, difference, 0.0)), 0.0)


def within_stretch(q_ref, k_ref, v_ref, rows_ref, cols_ref, scores_ref, within_ref):
    heads = q_ref.shape[0]
    for h in range(heads):
        decays = decays_of(rows_ref, cols_ref, heads, h)
        scores = (dot(q_ref[h], k_ref[h], 1, 1) * decays).astype(jnp.bfloat16)
        scores_ref[h] = scores
        within_ref[h] = dot(scores, v_ref[h], 1, 0)


def attend(q_ref, g_ref, state_ref, within_ref, cols_ref, att_ref, sums_ref):
    heads, tokens, width = q_ref.shape
    squares = crossed = jnp.zeros((tokens, width), jnp.float32)
    for h in range(heads):
        state = state_ref[h].astype(jnp.bfloat16)
        enter = cols_ref[:, heads + h : heads + h + 1]
        att = within_ref[h] + dot(q_ref[h], state, 1, 0) * enter
        att_ref[h] = att
        squares = squares + att * att
        crossed = crossed + g_ref[h].astype(jnp.float32) * att
    at = 0
    for terms in (squares, crossed):
        line = jnp.sum(terms.T, axis=0, keepdims=True)
        for start in range(0, tokens, width):
            piece = line[:, start : start + width]
            for p in range(sums_ref.shape[0]):
                sums_ref[p, at : at + 1] = piece
            at += 1


def normalise(features, q_ref, g_ref, att_ref, sums_ref, cols_ref, norm_ref, ga_ref, pay_ref, tmp_ref):
    heads, tokens, width = q_ref.shape
    per_head = ROW // heads
    depth = width // per_head
    lines = sums_ref.shape[1]
    tmp_ref[...] = jnp.zeros(tmp_ref.shape, jnp.float32)
    tmp_ref[0:lines] = jnp.sum(sums_ref[...], axis=0)
    upright = tmp_ref[...].T
    half = lines // 2
    squares = jnp.concatenate([upright[:, i : i + 1] for i in range(half)], axis=0)
    crossed = jnp.concatenate([upright[:, i : i + 1] for i in range(half, lines)], axis=0)
    mean = squares / features + EPSILON
    root = jnp.sqrt(mean)
    inverse = 1.0 / root
    factor = crossed / (features * root * root)
    for h in range(heads):
        att = att_ref[h]
        norm_ref[h] = (att * inverse).astype(jnp.bfloat16)
        ga = ((g_ref[h].astype(jnp.float32) - att * factor) * inverse).astype(jnp.bfloat16)
        ga_ref[h] = ga
        enter = cols_ref[:, heads + h : heads + h + 1]
        decayed = (q_ref[h].astype(jnp.float32) * enter).astype(jnp.bfloat16)
        back = dot(decayed, ga, 0, 0)
        for part in range(per_head):
            pay_ref[h * per_head + part] = back[part * depth : (part + 1) * depth]


def inner_gradients(
    q_ref, k_ref, v_ref, ga_ref, scores_ref, state_ref, rows_ref, cols_ref, gq_ref, ki_ref, vi_ref
):
    heads = q_ref.shape[0]
    for h in range(heads):
        ga = ga_ref[h]
        decays = decays_of(rows_ref, cols_ref, heads, h)
        slope = (dot(ga, v_ref[h], 1, 1) * decays).astype(jnp.bfloat16)
        enter = cols_ref[:, heads + h : heads + h + 1]
        state = state_ref[h].astype(jnp.bfloat16)
        gq_ref[h] = (dot(slope, k_ref[h], 1, 0) + dot(ga, state, 1, 1) * enter).astype(jnp.bfloat16)
        ki_ref[h] = dot(slope, q_ref[h], 0, 0)
        vi_ref[h] = dot(scores_ref[h], ga, 0, 0)


def outer_gradients(k_ref, v_ref, ki_ref, vi_ref, back_ref, cols_ref, gk_ref, gv_ref):
    heads = k_ref.shape[0]
    for h in range(heads):
        back = back_ref[h].astype(jnp.bfloat16)
        leave = cols_ref[:, 2 * heads + h : 2 * heads + h + 1]
        gk_ref[h] = (ki_ref[h] + dot(v_ref[h], back, 1, 1) * leave).astype(jnp.bfloat16)
        gv_ref[h] = (vi_ref[h] + dot(k_ref[h], back, 1, 0) * leave).astype(jnp.bfloat16)


def exchange(block, groups):
    return lax.all_to_all(
        block, "seq", split_axis=0, concat_axis=0, tiled=True, axis_index_groups=groups
    )


def passed_along(block, distance):
    devices = range(lax.axis_size("seq"))
    route = [(i, i + distance) for i in devices if i + distance in devices]
    return lax.ppermute(block, "seq", route)


def per_device(query_rows, key_rows, value_rows, log_gate, episode, grad_out):
    heads, tokens, width = query_rows.shape
    depth = heads * width // ROW
    devices = lax.axis_size("seq")
    groups = [list(range(at, at + ROW)) for at in range(0, devices, ROW)]
    f32, bf16 = jnp.float32, jnp.bfloat16
    block = (heads, tokens, width)
    product = 2 * heads * tokens * width * width
    square = 2 * heads * tokens * tokens * width
    line = 128

    pay, rows, cols = call(
        local_states,
        [
            ((ROW, depth + META, width), f32),
            ((line, tokens), f32),
            ((tokens, line), f32),
        ],
        product,
    )(log_gate, episode.reshape(1, tokens), key_rows, value_rows)
    got = exchange(pay, groups)
    total, facts = call(
        forward_row, [((depth + META, width), f32), ((ROW, META, width), f32)], got.size
    )(got)
    near = passed_along(total, ROW)
    scores, within = call(
        within_stretch, [((heads, tokens, tokens), bf16), (block, f32)], 2 * square
    )(query_rows, key_rows, value_rows, rows, cols)
    (states,) = call(forward_scan, [((ROW, depth, width), f32)], got.size)(got, facts, near)
    state = exchange(states, groups).reshape(heads, width, width)

    lines = 2 * tokens // width
    across = lax.axis_size("head")
    attention, sums = call(attend, [(block, f32), ((across, lines, width), f32)], product)(
        query_rows, grad_out, state, within, cols
    )
    sums = lax.all_to_all(sums, "head", split_axis=0, concat_axis=0, tiled=True)
    features = heads * across * width
    normed, grad_attn, pay = call(
        functools.partial(normalise, features),
        [(block, bf16), (block, bf16), ((ROW, depth, width), f32)],
        product,
        [pltpu.VMEM((width, width), f32)],
    )(query_rows, grad_out, attention, sums, cols)

    got = exchange(pay, groups)
    (total,) = call(backward_row, [((depth + META, width), f32)], got.size)(got, facts)
    near = passed_along(total, -ROW)
    query_grad, key_inner, value_inner = call(
        inner_gradients, [(block, bf16), (block, f32), (block, f32)], 4 * square + product
    )(query_rows, key_rows, value_rows, grad_attn, scores, state, rows, cols)
    (states,) = call(backward_scan, [((ROW, depth, width), f32)], got.size)(got, facts, near)
    back = exchange(states, groups).reshape(heads, width, width)
    key_grad, value_grad = call(outer_gradients, [(block, bf16), (block, bf16)], 2 * product)(
        key_rows, value_rows, key_inner, value_inner, back, cols
    )
    return normed, query_grad, key_grad, value_grad


def solution(mesh):
    rows = P("head", "seq", None)
    return jax.shard_map(
        per_device,
        mesh=mesh,
        in_specs=(rows, rows, rows, P("head", "seq"), P("seq"), rows),
        out_specs=(rows, rows, rows, rows),
        check_vma=False,
    )
```

time: 236 us -> 99 us (0.42)
  the two profiles are of different devices: /device:TPU:200 before, /device:TPU:136 now
where the time goes in v1:
time: 99 us; the launch traced here: 98.5 us
  blocking collectives  44.3 us (45%)
  waiting for transfers between devices  23.7 us (24%)
  starting transfers between devices  18.4 us (19%)
  Pallas kernels  8.03 us (8%)
  local copies, waits for them, and re-layouts  3.27 us (3%)
    all_to_all x2, blocking collectives, exchange(): lax.all_to_all(block, 'seq', split_axis=0, concat_axis=0, tiled=True, axi...  34.9 us
    all_to_all x2, waiting for transfers between devices, exchange(): lax.all_to_all(block, 'seq', split_axis=0, concat_axis=0, tiled=True, axi...  16.2 us
    all_to_all x1, blocking collectives, per_device(): sums = lax.all_to_all(sums, 'head', split_axis=0, concat_axis=0, tiled=True)  9.45 us
    ppermute x2, starting transfers between devices, passed_along(): return lax.ppermute(block, 'seq', route)  9.21 us
    all_to_all x2, starting transfers between devices, exchange(): lax.all_to_all(block, 'seq', split_axis=0, concat_axis=0, tiled=True, axi...  9.21 us
    pallas_call x10, Pallas kernels, run(): pl.pallas_call(body, out_shape=shapes, in_specs=[pl.BlockSpec(memory_spac...  8.03 us
    ppermute x2, waiting for transfers between devices, passed_along(): return lax.ppermute(block, 'seq', route)  7.58 us
    unnamed x16, local copies, waits for them, and re-layouts  3.27 us
  transfers between devices with their start and end apart: 4, of which 4 were waited for; matrix products, arithmetic and copies ran while one was open for 0% of the time, Pallas kernels for 3%

profile of v1, /device:TPU:136, one launch (start us, length us, event | category | flops | bytes accessed | tf_op | source)
XLA Modules:
  0.0 98.5 jit_solution(14341734375569179266)
XLA Ops:
  0.6 0.0 copy-start.7
  0.6 0.7 copy-done.7
  1.3 0.0 copy-start
  1.3 0.9 copy-done
  2.3 0.0 copy-start.2
  2.3 0.9 copy-done.2
  3.2 0.0 copy-start.6
  3.2 0.7 copy-done.6
  3.9 1.2 %local_states.1 = (f32[16,40,128]{2,1,0:T(8,128)S(1)}, f32[128,256]{1,0:T(8,128)S(1)}, f32[256,128]{1,0:T(8,128)S(1)}) custom-call(f32[4,256]{1,0:T(4,128)S(1)} %copy-done.6, s32[1,256]{1,0:T(1,128)S(1)} %bitcast.6, bf16[4,256,128]{2,1,0:T(8,128)(2,1)S(1)} %copy-done, bf16[4,256,128]{2,1,0:T(8,128)(2,1)S(1)} %copy-done.2), custom_call_target="tpu_custom_call" | custom-call | flops 33554432 | bytes 1119232 | tf_op jit(solution)/shard_map/local_states/pallas_call | solution.py:27
  5.1 20.5 %all_to_all.25.got_ref = f32[16,40,128]{2,1,0:T(8,128)S(1)} all-to-all(f32[16,40,128]{2,1,0:T(8,128)S(1)} %get-tuple-element.21), channel_id=1, replica_groups={{0,8,16,24,32,40,48,56,64,72,80,88,96,104,112,120},{128,136,144,152,160..., dimensions={0} | all-to-all | bytes 655360 | tf_op jit(solution)/shard_map/all_to_all | solution.py:221
  25.6 7.3 %collective-permute-start = (f32[40,128]{1,0:T(8,128)S(1)}, f32[40,128]{1,0:T(8,128)S(1)}, u32[]{:S(2)}, u32[]{:S(2)}) collective-permute-start(f32[40,128]{1,0:T(8,128)S(1)} %get-tuple-element.23), channel_id=1, source_target_pairs={{0,128},{8,136},{16,144},{24,152},{32,160},{40,168},{48,176},{56,1... | collective-permute-start | bytes 61448 | tf_op jit(solution)/shard_map/ppermute | solution.py:229
  32.9 1.5 %collective-permute-done.near_ref = f32[40,128]{1,0:T(8,128)S(1)} collective-permute-done((f32[40,128]{1,0:T(8,128)S(1)}, f32[40,128]{1,0:T(8,128)S(1)}, u32[]{:S(2)}, u32[]{:S(2)}) %collective-permute-start) | collective-permute-done | bytes 20512 | tf_op jit(solution)/shard_map/ppermute | solution.py:229
  34.4 0.0 copy-start.4
  34.4 0.8 forward_scan.1
  35.1 0.0 copy-start.1
  35.1 0.0 copy-start.3
  35.1 4.9 %all-to-all-start.1 = ((f32[16,32,128]{2,1,0:T(8,128)}), f32[16,32,128]{2,1,0:T(8,128)S(1)}, u32[]{:S(2)}, u32[]{:S(2)}) async-start(f32[16,32,128]{2,1,0:T(8,128)} %forward_scan.1), calls=%async_computation.1 | async-start | bytes 524288 | tf_op jit(solution)/shard_map/all_to_all | solution.py:221
  40.1 0.0 copy-done.4
  40.1 0.0 copy-done.1
  40.1 0.0 copy-done.3
  40.1 0.0 copy-start.5
  40.1 0.7 within_stretch.1
  40.8 8.7 %all-to-all-done.1 = f32[16,32,128]{2,1,0:T(8,128)S(1)} async-done(((f32[16,32,128]{2,1,0:T(8,128)}), f32[16,32,128]{2,1,0:T(8,128)S(1)}, u32[]{:S(2)}, u32[]{:S(2)}) %all-to-all-start.1) | async-done | bytes 262176 | tf_op jit(solution)/shard_map/all_to_all | solution.py:221
  49.5 0.0 copy-done.5
  49.5 0.4 attend.1
  49.9 9.5 %all_to_all.26.sums_ref = f32[8,4,128]{2,1,0:T(4,128)S(1)} all-to-all(f32[8,4,128]{2,1,0:T(4,128)S(1)} %get-tuple-element.28), channel_id=1, replica_groups=mesh['seq'=128,'head'=8] {'head'}, dimensions={0} | all-to-all | bytes 32768 | tf_op jit(solution)/shard_map/all_to_all | solution.py:268
  59.3 1.1 %normalise.1 = (bf16[4,256,128]{2,1,0:T(8,128)(2,1)}, bf16[4,256,128]{2,1,0:T(8,128)(2,1)S(1)}, f32[16,32,128]{2,1,0:T(8,128)S(1)}) custom-call(bf16[4,256,128]{2,1,0:T(8,128)(2,1)S(1)} %copy-done.4, bf16[4,256,128]{2,1,0:T(8,128)(2,1)S(1)} %copy-done.5, f32[4,256,128]{2,1,0:T(8,128)S(1)} %get-tuple-element.27.att_ref, ...), custom_call_target="tpu_custom_call" | custom-call | flops 33554432 | bytes 1982464 | tf_op jit(solution)/shard_map/normalise/pallas_call | solution.py:27
  60.4 14.4 %all_to_all.27.got_ref = f32[16,32,128]{2,1,0:T(8,128)S(1)} all-to-all(f32[16,32,128]{2,1,0:T(8,128)S(1)} %get-tuple-element.35), channel_id=1, replica_groups={{0,8,16,24,32,40,48,56,64,72,80,88,96,104,112,120},{128,136,144,152,160..., dimensions={0} | all-to-all | bytes 524288 | tf_op jit(solution)/shard_map/all_to_all | solution.py:221
  74.9 1.9 %collective-permute-start.1 = (f32[40,128]{1,0:T(8,128)S(1)}, f32[40,128]{1,0:T(8,128)S(1)}, u32[]{:S(2)}, u32[]{:S(2)}) collective-permute-start(f32[40,128]{1,0:T(8,128)S(1)} %backward_row.1), channel_id=1, source_target_pairs={{128,0},{136,8},{144,16},{152,24},{160,32},{168,40},{176,48},{184,... | collective-permute-start | bytes 61448 | tf_op jit(solution)/shard_map/ppermute | solution.py:229
  76.8 6.1 %collective-permute-done.1.near_ref = f32[40,128]{1,0:T(8,128)S(1)} collective-permute-done((f32[40,128]{1,0:T(8,128)S(1)}, f32[40,128]{1,0:T(8,128)S(1)}, u32[]{:S(2)}, u32[]{:S(2)}) %collective-permute-start.1) | collective-permute-done | bytes 20512 | tf_op jit(solution)/shard_map/ppermute | solution.py:229
  82.9 0.8 backward_scan.1
  83.7 4.3 %all-to-all-start.4 = ((f32[16,32,128]{2,1,0:T(8,128)}), f32[16,32,128]{2,1,0:T(8,128)S(1)}, u32[]{:S(2)}, u32[]{:S(2)}) async-start(f32[16,32,128]{2,1,0:T(8,128)} %backward_scan.1), calls=%async_computation.4 | async-start | bytes 524288 | tf_op jit(solution)/shard_map/all_to_all | solution.py:221
  87.9 2.0 %inner_gradients.1 = (bf16[4,256,128]{2,1,0:T(8,128)(2,1)}, f32[4,256,128]{2,1,0:T(8,128)S(1)}, f32[4,256,128]{2,1,0:T(8,128)S(1)}) custom-call(bf16[4,256,128]{2,1,0:T(8,128)(2,1)S(1)} %copy-done.4, bf16[4,256,128]{2,1,0:T(8,128)(2,1)S(1)} %copy-done.1, bf16[4,256,128]{2,1,0:T(8,128)(2,1)S(1)} %copy-done.3, ...), custom_call_target="tpu_custom_call" | custom-call | flops 301989888 | bytes 3407872 | tf_op jit(solution)/shard_map/inner_gradients/pallas_call | solution.py:27
  90.0 7.4 %all-to-all-done.4 = f32[16,32,128]{2,1,0:T(8,128)S(1)} async-done(((f32[16,32,128]{2,1,0:T(8,128)}), f32[16,32,128]{2,1,0:T(8,128)S(1)}, u32[]{:S(2)}, u32[]{:S(2)}) %all-to-all-start.4) | async-done | bytes 262176 | tf_op jit(solution)/shard_map/all_to_all | solution.py:221
  97.4 1.1 %outer_gradients.1 = (bf16[4,256,128]{2,1,0:T(8,128)(2,1)}, bf16[4,256,128]{2,1,0:T(8,128)(2,1)}) custom-call(bf16[4,256,128]{2,1,0:T(8,128)(2,1)S(1)} %copy-done.1, bf16[4,256,128]{2,1,0:T(8,128)(2,1)S(1)} %copy-done.3, f32[4,256,128]{2,1,0:T(8,128)S(1)} %get-tuple-element.33.ki_ref, f32[4,256,128]{2,1,0:T(8,128)S(1)} %get-tuple-element.34.vi_ref, ...), custom_call_target="tpu_custom_call" | custom-call | flops 67108864 | bytes 2490368 | tf_op jit(solution)/shard_map/outer_gradients/pallas_call | solution.py:27
  (2 shorter events, 0.1 us)
Async XLA Ops:
  0.6 0.7 copy-start.7
  1.3 0.9 copy-start
  2.3 0.9 copy-start.2
  3.2 0.7 copy-start.6
  25.6 8.8 %collective-permute-start = (f32[40,128]{1,0:T(8,128)S(1)}, f32[40,128]{1,0:T(8,128)S(1)}, u32[]{:S(2)}, u32[]{:S(2)}) collective-permute-start(f32[40,128]{1,0:T(8,128)S(1)} %get-tuple-element.23), channel_id=1, source_target_pairs={{0,128},{8,136},{16,144},{24,152},{32,160},{40,168},{48,176},{56,1... | collective-permute-start | bytes 61448 | tf_op jit(solution)/shard_map/ppermute | solution.py:229
  34.4 5.7 %copy-start.4 = (bf16[4,256,128]{2,1,0:T(8,128)(2,1)S(1)}, bf16[4,256,128]{2,1,0:T(8,128)(2,1)}, u32[]{:S(2)}) copy-start(bf16[4,256,128]{2,1,0:T(8,128)(2,1)} %q_ref.7) | copy-start | bytes 786436
  35.1 4.9 %copy-start.1 = (bf16[4,256,128]{2,1,0:T(8,128)(2,1)S(1)}, bf16[4,256,128]{2,1,0:T(8,128)(2,1)}, u32[]{:S(2)}) copy-start(bf16[4,256,128]{2,1,0:T(8,128)(2,1)} %k_ref.7) | copy-start | bytes 786436
  35.1 4.9 %copy-start.3 = (bf16[4,256,128]{2,1,0:T(8,128)(2,1)S(1)}, bf16[4,256,128]{2,1,0:T(8,128)(2,1)}, u32[]{:S(2)}) copy-start(bf16[4,256,128]{2,1,0:T(8,128)(2,1)} %v_ref.7) | copy-start | bytes 786436
  35.1 14.3 %all-to-all-start.1 = ((f32[16,32,128]{2,1,0:T(8,128)}), f32[16,32,128]{2,1,0:T(8,128)S(1)}, u32[]{:S(2)}, u32[]{:S(2)}) async-start(f32[16,32,128]{2,1,0:T(8,128)} %forward_scan.1), calls=%async_computation.1 | async-start | bytes 524288 | tf_op jit(solution)/shard_map/all_to_all | solution.py:221
  40.1 9.4 %copy-start.5 = (bf16[4,256,128]{2,1,0:T(8,128)(2,1)S(1)}, bf16[4,256,128]{2,1,0:T(8,128)(2,1)}, u32[]{:S(2)}) copy-start(bf16[4,256,128]{2,1,0:T(8,128)(2,1)} %g_ref.3) | copy-start | bytes 786436
  74.9 8.0 %collective-permute-start.1 = (f32[40,128]{1,0:T(8,128)S(1)}, f32[40,128]{1,0:T(8,128)S(1)}, u32[]{:S(2)}, u32[]{:S(2)}) collective-permute-start(f32[40,128]{1,0:T(8,128)S(1)} %backward_row.1), channel_id=1, source_target_pairs={{128,0},{136,8},{144,16},{152,24},{160,32},{168,40},{176,48},{184,... | collective-permute-start | bytes 61448 | tf_op jit(solution)/shard_map/ppermute | solution.py:229
  83.7 13.8 %all-to-all-start.4 = ((f32[16,32,128]{2,1,0:T(8,128)}), f32[16,32,128]{2,1,0:T(8,128)S(1)}, u32[]{:S(2)}, u32[]{:S(2)}) async-start(f32[16,32,128]{2,1,0:T(8,128)} %backward_scan.1), calls=%async_computation.4 | async-start | bytes 524288 | tf_op jit(solution)/shard_map/all_to_all | solution.py:221

commit v2 on v1

--- a/solution.py
+++ b/solution.py
@@ -19,7 +19,7 @@
     )
 
 
-def call(body, outs, flops, scratch=()):
+def call(body, outs, flops, scratch=(), from_hbm=False, to_hbm=False):
     shapes = [jax.ShapeDtypeStruct(s, d) for s, d in outs]
 
     def run(*args):
@@ -27,8 +27,8 @@
         return pl.pallas_call(
             body,
             out_shape=shapes,
-            in_specs=[pl.BlockSpec(memory_space=pltpu.VMEM)] * len(args),
-            out_specs=[pl.BlockSpec(memory_space=pltpu.VMEM)] * len(shapes),
+            in_specs=[pl.BlockSpec(memory_space=pltpu.HBM if from_hbm else pltpu.VMEM)] * len(args),
+            out_specs=[pl.BlockSpec(memory_space=pltpu.HBM if to_hbm else pltpu.VMEM)] * len(shapes),
             scratch_shapes=list(scratch),
             cost_estimate=pl.CostEstimate(flops=flops, bytes_accessed=size, transcendentals=0),
             compiler_params=pltpu.CompilerParams(vmem_limit_bytes=8 << 20),
@@ -38,11 +38,24 @@
     return run
 
 
-def local_states(gate_ref, ep_ref, k_ref, v_ref, pay_ref, rows_ref, cols_ref):
+def local_states(
+    gate_hbm, ep_hbm, k_hbm, v_hbm, pay_ref, rows_ref, cols_ref, gate_ref, ep_ref, k_ref, v_ref, sems
+):
     heads, tokens = gate_ref.shape
     width = k_ref.shape[2]
     per_head = ROW // heads
     depth = width // per_head
+    gates = pltpu.make_async_copy(gate_hbm, gate_ref, sems.at[0])
+    ids = pltpu.make_async_copy(ep_hbm, ep_ref, sems.at[1])
+    gates.start()
+    ids.start()
+    keys, values = [], []
+    for h in range(heads):
+        keys.append(pltpu.make_async_copy(k_hbm.at[h], k_ref.at[h], sems.at[2 + h]))
+        values.append(pltpu.make_async_copy(v_hbm.at[h], v_ref.at[h], sems.at[2 + heads + h]))
+        keys[h].start()
+        values[h].start()
+    gates.wait()
     run = gate_ref[...]
     place = lax.broadcasted_iota(jnp.int32, run.shape, 1)
     step = 1
@@ -50,6 +63,7 @@
         run = run + jnp.where(place >= step, pltpu.roll(run, step, 1), 0.0)
         step *= 2
     total = run[:, tokens - 1 :]
+    ids.wait()
     ep = ep_ref[...]
     first, last = ep[:, :1], ep[:, tokens - 1 :]
     rows_ref[...] = jnp.zeros(rows_ref.shape, jnp.float32)
@@ -61,6 +75,8 @@
     fact = lax.broadcasted_iota(jnp.int32, (META, width), 0)
     first_f, last_f = first.astype(jnp.float32), last.astype(jnp.float32)
     for h in range(heads):
+        keys[h].wait()
+        values[h].wait()
         leave = cols_ref[:, 2 * heads + h : 2 * heads + h + 1]
         decayed = (k_ref[h].astype(jnp.float32) * leave).astype(jnp.bfloat16)
         state = dot(decayed, v_ref[h], 0, 0)
@@ -166,10 +182,7 @@
             at += 1
 
 
-def normalise(features, q_ref, g_ref, att_ref, sums_ref, cols_ref, norm_ref, ga_ref, pay_ref, tmp_ref):
-    heads, tokens, width = q_ref.shape
-    per_head = ROW // heads
-    depth = width // per_head
+def token_scales(features, sums_ref, tmp_ref):
     lines = sums_ref.shape[1]
     tmp_ref[...] = jnp.zeros(tmp_ref.shape, jnp.float32)
     tmp_ref[0:lines] = jnp.sum(sums_ref[...], axis=0)
@@ -177,14 +190,20 @@
     half = lines // 2
     squares = jnp.concatenate([upright[:, i : i + 1] for i in range(half)], axis=0)
     crossed = jnp.concatenate([upright[:, i : i + 1] for i in range(half, lines)], axis=0)
-    mean = squares / features + EPSILON
-    root = jnp.sqrt(mean)
-    inverse = 1.0 / root
-    factor = crossed / (features * root * root)
-    for h in range(heads):
-        att = att_ref[h]
-        norm_ref[h] = (att * inverse).astype(jnp.bfloat16)
-        ga = ((g_ref[h].astype(jnp.float32) - att * factor) * inverse).astype(jnp.bfloat16)
+    root = jnp.sqrt(squares / features + EPSILON)
+    return 1.0 / root, crossed / (features * root * root)
+
+
+def own_gradient_state(
+    features, q_ref, g_ref, att_ref, sums_ref, cols_ref, ga_ref, pay_ref, scale_ref, tmp_ref
+):
+    heads, tokens, width = q_ref.shape
+    per_head = ROW // heads
+    depth = width // per_head
+    inverse, factor = token_scales(features, sums_ref, tmp_ref)
+    scale_ref[...] = jnp.broadcast_to(inverse, scale_ref.shape)
+    for h in range(heads):
+        ga = ((g_ref[h].astype(jnp.float32) - att_ref[h] * factor) * inverse).astype(jnp.bfloat16)
         ga_ref[h] = ga
         enter = cols_ref[:, heads + h : heads + h + 1]
         decayed = (q_ref[h].astype(jnp.float32) * enter).astype(jnp.bfloat16)
@@ -194,10 +213,24 @@
 
 
 def inner_gradients(
-    q_ref, k_ref, v_ref, ga_ref, scores_ref, state_ref, rows_ref, cols_ref, gq_ref, ki_ref, vi_ref
+    q_ref,
+    k_ref,
+    v_ref,
+    ga_ref,
+    scores_ref,
+    state_ref,
+    rows_ref,
+    cols_ref,
+    att_ref,
+    scale_ref,
+    norm_ref,
+    gq_ref,
+    ki_ref,
+    vi_ref,
 ):
     heads = q_ref.shape[0]
     for h in range(heads):
+        norm_ref[h] = (att_ref[h] * scale_ref[...]).astype(jnp.bfloat16)
         ga = ga_ref[h]
         decays = decays_of(rows_ref, cols_ref, heads, h)
         slope = (dot(ga, v_ref[h], 1, 1) * decays).astype(jnp.bfloat16)
@@ -208,13 +241,26 @@
         vi_ref[h] = dot(scores_ref[h], ga, 0, 0)
 
 
-def outer_gradients(k_ref, v_ref, ki_ref, vi_ref, back_ref, cols_ref, gk_ref, gv_ref):
+def outer_gradients(
+    k_ref, v_ref, ki_ref, vi_ref, back_ref, cols_ref, gk_hbm, gv_hbm, gk_ref, gv_ref, sems
+):
     heads = k_ref.shape[0]
+    copies = []
     for h in range(heads):
         back = back_ref[h].astype(jnp.bfloat16)
         leave = cols_ref[:, 2 * heads + h : 2 * heads + h + 1]
         gk_ref[h] = (ki_ref[h] + dot(v_ref[h], back, 1, 1) * leave).astype(jnp.bfloat16)
+        copies.append(pltpu.make_async_copy(gk_ref.at[h], gk_hbm.at[h], sems.at[2 * h]))
+        copies[-1].start()
         gv_ref[h] = (vi_ref[h] + dot(k_ref[h], back, 1, 0) * leave).astype(jnp.bfloat16)
+        copies.append(pltpu.make_async_copy(gv_ref.at[h], gv_hbm.at[h], sems.at[2 * h + 1]))
+        copies[-1].start()
+    for copy in copies:
+        copy.wait()
+
+
+def in_hbm(array):
+    return pltpu.with_memory_space_constraint(array, pltpu.HBM)
 
 
 def exchange(block, groups):
@@ -248,7 +294,15 @@
             ((tokens, line), f32),
         ],
         product,
-    )(log_gate, episode.reshape(1, tokens), key_rows, value_rows)
+        [
+            pltpu.VMEM((heads, tokens), f32),
+            pltpu.VMEM((1, tokens), jnp.int32),
+            pltpu.VMEM(block, bf16),
+            pltpu.VMEM(block, bf16),
+            pltpu.SemaphoreType.DMA((2 + 2 * heads,)),
+        ],
+        from_hbm=True,
+    )(*map(in_hbm, (log_gate, episode.reshape(1, tokens), key_rows, value_rows)))
     got = exchange(pay, groups)
     total, facts = call(
         forward_row, [((depth + META, width), f32), ((ROW, META, width), f32)], got.size
@@ -257,6 +311,7 @@
     scores, within = call(
         within_stretch, [((heads, tokens, tokens), bf16), (block, f32)], 2 * square
     )(query_rows, key_rows, value_rows, rows, cols)
+    near, scores, within = lax.optimization_barrier((near, scores, within))
     (states,) = call(forward_scan, [((ROW, depth, width), f32)], got.size)(got, facts, near)
     state = exchange(states, groups).reshape(heads, width, width)
 
@@ -267,9 +322,9 @@
     )
     sums = lax.all_to_all(sums, "head", split_axis=0, concat_axis=0, tiled=True)
     features = heads * across * width
-    normed, grad_attn, pay = call(
-        functools.partial(normalise, features),
-        [(block, bf16), (block, bf16), ((ROW, depth, width), f32)],
+    grad_attn, pay, scale = call(
+        functools.partial(own_gradient_state, features),
+        [(block, bf16), ((ROW, depth, width), f32), ((tokens, width), f32)],
         product,
         [pltpu.VMEM((width, width), f32)],
     )(query_rows, grad_out, attention, sums, cols)
@@ -277,14 +332,36 @@
     got = exchange(pay, groups)
     (total,) = call(backward_row, [((depth + META, width), f32)], got.size)(got, facts)
     near = passed_along(total, -ROW)
-    query_grad, key_inner, value_inner = call(
-        inner_gradients, [(block, bf16), (block, f32), (block, f32)], 4 * square + product
-    )(query_rows, key_rows, value_rows, grad_attn, scores, state, rows, cols)
+    normed, query_grad, key_inner, value_inner = call(
+        inner_gradients,
+        [(block, bf16), (block, bf16), (block, f32), (block, f32)],
+        4 * square + product,
+    )(
+        query_rows,
+        key_rows,
+        value_rows,
+        grad_attn,
+        scores,
+        state,
+        rows,
+        cols,
+        attention,
+        scale,
+    )
+    near, key_inner, value_inner = lax.optimization_barrier((near, key_inner, value_inner))
     (states,) = call(backward_scan, [((ROW, depth, width), f32)], got.size)(got, facts, near)
     back = exchange(states, groups).reshape(heads, width, width)
-    key_grad, value_grad = call(outer_gradients, [(block, bf16), (block, bf16)], 2 * product)(
-        key_rows, value_rows, key_inner, value_inner, back, cols
-    )
+    key_grad, value_grad = call(
+        outer_gradients,
+        [(block, bf16), (block, bf16)],
+        2 * product,
+        [
+            pltpu.VMEM(block, bf16),
+            pltpu.VMEM(block, bf16),
+            pltpu.SemaphoreType.DMA((2 * heads,)),
+        ],
+        to_hbm=True,
+    )(key_rows, value_rows, key_inner, value_inner, back, cols)
     return normed, query_grad, key_grad, value_grad
 
 

time: 99 us -> 95.2 us (0.962)
  blocking collectives: 44.3 us -> 72.1 us
  waiting for transfers between devices: 23.7 us -> 4.75 us
  starting transfers between devices: 18.4 us -> 9.35 us
  local copies, waits for them, and re-layouts: 3.27 us -> 0.02 us
    all_to_all x2 -> x4, blocking collectives: 34.9 us -> 62.7 us  [exchange(): lax.all_to_all(block, 'seq', split_axis=0, concat_axis=0, tiled=True, axi...]
    all_to_all x2 -> x0, waiting for transfers between devices: 16.2 us -> none  [exchange(): lax.all_to_all(block, 'seq', split_axis=0, concat_axis=0, tiled=True, axi...]
    all_to_all x2 -> x0, starting transfers between devices: 9.21 us -> none  [exchange(): lax.all_to_all(block, 'seq', split_axis=0, concat_axis=0, tiled=True, axi...]
    unnamed x16 -> x8, local copies, waits for them, and re-layouts: 3.27 us -> 0.02 us
    ppermute x2, waiting for transfers between devices: 7.58 us -> 4.75 us  [passed_along(): return lax.ppermute(block, 'seq', route)]
  transfers between devices with their start and end apart: 4 -> 2, of which waited for: 4 -> 2; matrix products, arithmetic and copies ran while one was open for 0% -> 0% of each run, Pallas kernels for 3% -> 3%
where the time goes in v2:
time: 95.2 us; the launch traced here: 94.8 us
  blocking collectives  72.1 us (76%)
  starting transfers between devices  9.35 us (10%)
  Pallas kernels  7.84 us (8%)
  waiting for transfers between devices  4.75 us (5%)
    all_to_all x4, blocking collectives, exchange(): lax.all_to_all(block, 'seq', split_axis=0, concat_axis=0, tiled=True, axi...  62.7 us
    all_to_all x1, blocking collectives, per_device(): sums = lax.all_to_all(sums, 'head', split_axis=0, concat_axis=0, tiled=True)  9.46 us
    ppermute x2, starting transfers between devices, passed_along(): return lax.ppermute(block, 'seq', route)  9.35 us
    pallas_call x10, Pallas kernels, run(): pl.pallas_call(body, out_shape=shapes, in_specs=[pl.BlockSpec(memory_spac...  7.84 us
    ppermute x2, waiting for transfers between devices, passed_along(): return lax.ppermute(block, 'seq', route)  4.75 us
  transfers between devices with their start and end apart: 2, of which 2 were waited for; matrix products, arithmetic and copies ran while one was open for 0% of the time, Pallas kernels for 3%

profile of v2, /device:TPU:136, one launch (start us, length us, event | category | flops | bytes accessed | tf_op | source)
XLA Modules:
  0.0 94.8 jit_solution(2541275040958197696)
XLA Ops:
  0.6 2.6 %local_states.1 = (f32[16,40,128]{2,1,0:T(8,128)S(1)}, f32[128,256]{1,0:T(8,128)S(1)}, f32[256,128]{1,0:T(8,128)S(1)}) custom-call(f32[4,256]{1,0:T(4,128)} %gate_hbm.1, s32[1,256]{1,0:T(1,128)} %bitcast.6, bf16[4,256,128]{2,1,0:T(8,128)(2,1)} %k_ref.5, bf16[4,256,128]{2,1,0:T(8,128)(2,1)} %v_ref.5), custom_call_target="tpu_custom_call" | custom-call | flops 33554432 | bytes 1119232 | tf_op jit(solution)/shard_map/local_states/pallas_call | solution.py:27
  3.3 0.0 copy-start.1
  3.3 0.0 copy-start.2
  3.3 20.6 %all_to_all.25.got_ref = f32[16,40,128]{2,1,0:T(8,128)S(1)} all-to-all(f32[16,40,128]{2,1,0:T(8,128)S(1)} %get-tuple-element.28), channel_id=1, replica_groups={{0,8,16,24,32,40,48,56,64,72,80,88,96,104,112,120},{128,136,144,152,160..., dimensions={0} | all-to-all | bytes 655360 | tf_op jit(solution)/shard_map/all_to_all | solution.py:267
  23.9 0.0 copy-start
  24.0 7.4 %collective-permute-start = (f32[40,128]{1,0:T(8,128)S(1)}, f32[40,128]{1,0:T(8,128)S(1)}, u32[]{:S(2)}, u32[]{:S(2)}) collective-permute-start(f32[40,128]{1,0:T(8,128)S(1)} %get-tuple-element.30), channel_id=1, source_target_pairs={{0,128},{8,136},{16,144},{24,152},{32,160},{40,168},{48,176},{56,1... | collective-permute-start | bytes 61448 | tf_op jit(solution)/shard_map/ppermute | solution.py:275
  31.4 0.0 copy-done.1
  31.4 0.0 copy-done.2
  31.4 0.0 copy-done
  31.4 0.7 within_stretch.1
  32.1 0.8 collective-permute-done.near_ref
  32.9 0.1 forward_scan.1
  32.9 0.0 copy-start.3
  32.9 14.1 %all_to_all.26 = f32[16,32,128]{2,1,0:T(8,128)S(1)} all-to-all(f32[16,32,128]{2,1,0:T(8,128)S(1)} %forward_scan.1), channel_id=1, replica_groups={{0,8,16,24,32,40,48,56,64,72,80,88,96,104,112,120},{128,136,144,152,160..., dimensions={0} | all-to-all | bytes 524288 | tf_op jit(solution)/shard_map/all_to_all | solution.py:267
  47.1 0.0 copy-done.3
  47.1 0.4 attend.1
  47.5 9.5 %all_to_all.27.sums_ref = f32[8,4,128]{2,1,0:T(4,128)S(1)} all-to-all(f32[8,4,128]{2,1,0:T(4,128)S(1)} %get-tuple-element.38), channel_id=1, replica_groups=mesh['seq'=128,'head'=8] {'head'}, dimensions={0} | all-to-all | bytes 32768 | tf_op jit(solution)/shard_map/all_to_all | solution.py:323
  56.9 0.8 own_gradient_state.1
  57.7 14.4 %all_to_all.28.got_ref = f32[16,32,128]{2,1,0:T(8,128)S(1)} all-to-all(f32[16,32,128]{2,1,0:T(8,128)S(1)} %get-tuple-element.44), channel_id=1, replica_groups={{0,8,16,24,32,40,48,56,64,72,80,88,96,104,112,120},{128,136,144,152,160..., dimensions={0} | all-to-all | bytes 524288 | tf_op jit(solution)/shard_map/all_to_all | solution.py:267
  72.1 1.9 %collective-permute-start.1 = (f32[40,128]{1,0:T(8,128)S(1)}, f32[40,128]{1,0:T(8,128)S(1)}, u32[]{:S(2)}, u32[]{:S(2)}) collective-permute-start(f32[40,128]{1,0:T(8,128)S(1)} %backward_row.1), channel_id=1, source_target_pairs={{128,0},{136,8},{144,16},{152,24},{160,32},{168,40},{176,48},{184,... | collective-permute-start | bytes 61448 | tf_op jit(solution)/shard_map/ppermute | solution.py:275
  74.1 2.1 %inner_gradients.1 = (bf16[4,256,128]{2,1,0:T(8,128)(2,1)}, bf16[4,256,128]{2,1,0:T(8,128)(2,1)}, f32[4,256,128]{2,1,0:T(8,128)S(1)}, f32[4,256,128]{2,1,0:T(8,128)S(1)}) custom-call(bf16[4,256,128]{2,1,0:T(8,128)(2,1)S(1)} %copy-done.2, bf16[4,256,128]{2,1,0:T(8,128)(2,1)S(1)} %copy-done, bf16[4,256,128]{2,1,0:T(8,128)(2,1)S(1)} %copy-done.1, ...), custom_call_target="tpu_custom_call" | custom-call | flops 301989888 | bytes 4325376 | tf_op jit(solution)/shard_map/inner_gradients/pallas_call | solution.py:27
  76.2 4.0 %collective-permute-done.1.near_ref = f32[40,128]{1,0:T(8,128)S(1)} collective-permute-done((f32[40,128]{1,0:T(8,128)S(1)}, f32[40,128]{1,0:T(8,128)S(1)}, u32[]{:S(2)}, u32[]{:S(2)}) %collective-permute-start.1) | collective-permute-done | bytes 20512 | tf_op jit(solution)/shard_map/ppermute | solution.py:275
  80.2 13.6 %all_to_all.29 = f32[16,32,128]{2,1,0:T(8,128)S(1)} all-to-all(f32[16,32,128]{2,1,0:T(8,128)S(1)} %backward_scan.1), channel_id=1, replica_groups={{0,8,16,24,32,40,48,56,64,72,80,88,96,104,112,120},{128,136,144,152,160..., dimensions={0} | all-to-all | bytes 524288 | tf_op jit(solution)/shard_map/all_to_all | solution.py:267
  93.8 1.0 %outer_gradients.1 = (bf16[4,256,128]{2,1,0:T(8,128)(2,1)}, bf16[4,256,128]{2,1,0:T(8,128)(2,1)}) custom-call(bf16[4,256,128]{2,1,0:T(8,128)(2,1)S(1)} %copy-done, bf16[4,256,128]{2,1,0:T(8,128)(2,1)S(1)} %copy-done.1, f32[4,256,128]{2,1,0:T(8,128)S(1)} %get-tuple-element.47.ki_ref, f32[4,256,128]{2,1,0:T(8,128)S(1)} %get-tuple-element.48.vi_ref, ...), custom_call_target="tpu_custom_call" | custom-call | flops 67108864 | bytes 2490368 | tf_op jit(solution)/shard_map/outer_gradients/pallas_call | solution.py:27
  (3 shorter events, 0.1 us)
Async XLA Ops:
  3.3 28.1 %copy-start.1 = (bf16[4,256,128]{2,1,0:T(8,128)(2,1)S(1)}, bf16[4,256,128]{2,1,0:T(8,128)(2,1)}, u32[]{:S(2)}) copy-start(bf16[4,256,128]{2,1,0:T(8,128)(2,1)} %v_ref.5) | copy-start | bytes 786436
  3.3 28.1 %copy-start.2 = (bf16[4,256,128]{2,1,0:T(8,128)(2,1)S(1)}, bf16[4,256,128]{2,1,0:T(8,128)(2,1)}, u32[]{:S(2)}) copy-start(bf16[4,256,128]{2,1,0:T(8,128)(2,1)} %q_ref.7) | copy-start | bytes 786436
  23.9 7.5 %copy-start = (bf16[4,256,128]{2,1,0:T(8,128)(2,1)S(1)}, bf16[4,256,128]{2,1,0:T(8,128)(2,1)}, u32[]{:S(2)}) copy-start(bf16[4,256,128]{2,1,0:T(8,128)(2,1)} %k_ref.5) | copy-start | bytes 786436
  24.0 8.9 %collective-permute-start = (f32[40,128]{1,0:T(8,128)S(1)}, f32[40,128]{1,0:T(8,128)S(1)}, u32[]{:S(2)}, u32[]{:S(2)}) collective-permute-start(f32[40,128]{1,0:T(8,128)S(1)} %get-tuple-element.30), channel_id=1, source_target_pairs={{0,128},{8,136},{16,144},{24,152},{32,160},{40,168},{48,176},{56,1... | collective-permute-start | bytes 61448 | tf_op jit(solution)/shard_map/ppermute | solution.py:275
  32.9 14.1 %copy-start.3 = (bf16[4,256,128]{2,1,0:T(8,128)(2,1)S(1)}, bf16[4,256,128]{2,1,0:T(8,128)(2,1)}, u32[]{:S(2)}) copy-start(bf16[4,256,128]{2,1,0:T(8,128)(2,1)} %g_ref.3) | copy-start | bytes 786436
  72.1 8.0 %collective-permute-start.1 = (f32[40,128]{1,0:T(8,128)S(1)}, f32[40,128]{1,0:T(8,128)S(1)}, u32[]{:S(2)}, u32[]{:S(2)}) collective-permute-start(f32[40,128]{1,0:T(8,128)S(1)} %backward_row.1), channel_id=1, source_target_pairs={{128,0},{136,8},{144,16},{152,24},{160,32},{168,40},{176,48},{184,... | collective-permute-start | bytes 61448 | tf_op jit(solution)/shard_map/ppermute | solution.py:275

commit v3 on v2

--- a/solution.py
+++ b/solution.py
@@ -38,8 +38,16 @@
     return run
 
 
+def running_sums(gates, ones):
+    high = gates.astype(jnp.bfloat16)
+    rest = gates - high.astype(jnp.float32)
+    middle = rest.astype(jnp.bfloat16)
+    low = (rest - middle.astype(jnp.float32)).astype(jnp.bfloat16)
+    return dot(low, ones, 1, 0) + dot(middle, ones, 1, 0) + dot(high, ones, 1, 0)
+
+
 def local_states(
-    gate_hbm, ep_hbm, k_hbm, v_hbm, pay_ref, rows_ref, cols_ref, gate_ref, ep_ref, k_ref, v_ref, sems
+    gate_hbm, ep_hbm, k_hbm, v_hbm, pay_ref, rows_ref, gate_ref, ep_ref, k_ref, v_ref, sems
 ):
     heads, tokens = gate_ref.shape
     width = k_ref.shape[2]
@@ -49,37 +57,35 @@
     ids = pltpu.make_async_copy(ep_hbm, ep_ref, sems.at[1])
     gates.start()
     ids.start()
-    keys, values = [], []
-    for h in range(heads):
-        keys.append(pltpu.make_async_copy(k_hbm.at[h], k_ref.at[h], sems.at[2 + h]))
-        values.append(pltpu.make_async_copy(v_hbm.at[h], v_ref.at[h], sems.at[2 + heads + h]))
-        keys[h].start()
-        values[h].start()
+    keys = [pltpu.make_async_copy(k_hbm.at[h], k_ref.at[h], sems.at[2 + h]) for h in range(heads)]
+    values = [
+        pltpu.make_async_copy(v_hbm.at[h], v_ref.at[h], sems.at[2 + heads + h])
+        for h in range(heads)
+    ]
+    for copy in (*keys, *values):
+        copy.start()
+    rows_ref[...] = jnp.zeros(rows_ref.shape, jnp.float32)
+    upto = lax.broadcasted_iota(jnp.int32, (tokens, tokens), 0)
+    place = lax.broadcasted_iota(jnp.int32, (tokens, tokens), 1)
+    ones = jnp.where(upto <= place, 1.0, 0.0).astype(jnp.bfloat16)
     gates.wait()
-    run = gate_ref[...]
-    place = lax.broadcasted_iota(jnp.int32, run.shape, 1)
-    step = 1
-    while step < tokens:
-        run = run + jnp.where(place >= step, pltpu.roll(run, step, 1), 0.0)
-        step *= 2
+    run = running_sums(gate_ref[...], ones)
     total = run[:, tokens - 1 :]
     ids.wait()
     ep = ep_ref[...]
     first, last = ep[:, :1], ep[:, tokens - 1 :]
-    rows_ref[...] = jnp.zeros(rows_ref.shape, jnp.float32)
+    leave = jnp.where(ep == last, jnp.exp(total - run), 0.0)
     rows_ref[0:heads] = run
     rows_ref[heads : 2 * heads] = jnp.where(ep == first, jnp.exp(run), 0.0)
-    rows_ref[2 * heads : 3 * heads] = jnp.where(ep == last, jnp.exp(total - run), 0.0)
+    rows_ref[2 * heads : 3 * heads] = leave
     rows_ref[3 * heads : 3 * heads + 1] = ep.astype(jnp.float32)
-    cols_ref[...] = rows_ref[...].T
     fact = lax.broadcasted_iota(jnp.int32, (META, width), 0)
     first_f, last_f = first.astype(jnp.float32), last.astype(jnp.float32)
     for h in range(heads):
         keys[h].wait()
+        decayed = (k_ref[h].T.astype(jnp.float32) * leave[h : h + 1]).astype(jnp.bfloat16)
         values[h].wait()
-        leave = cols_ref[:, 2 * heads + h : 2 * heads + h + 1]
-        decayed = (k_ref[h].astype(jnp.float32) * leave).astype(jnp.bfloat16)
-        state = dot(decayed, v_ref[h], 0, 0)
+        state = dot(decayed, v_ref[h], 1, 0)
         facts = jnp.where(
             fact == 0,
             total[h : h + 1],
@@ -153,13 +159,18 @@
     return jnp.where(allowed, jnp.exp(jnp.where(allowed, difference, 0.0)), 0.0)
 
 
-def within_stretch(q_ref, k_ref, v_ref, rows_ref, cols_ref, scores_ref, within_ref):
+def within_stretch(
+    q_ref, k_ref, v_ref, rows_ref, scores_ref, within_ref, decayed_ref, cols_ref
+):
     heads = q_ref.shape[0]
+    cols_ref[...] = rows_ref[...].T
     for h in range(heads):
         decays = decays_of(rows_ref, cols_ref, heads, h)
         scores = (dot(q_ref[h], k_ref[h], 1, 1) * decays).astype(jnp.bfloat16)
         scores_ref[h] = scores
         within_ref[h] = dot(scores, v_ref[h], 1, 0)
+        enter = rows_ref[heads + h : heads + h + 1]
+        decayed_ref[h] = (q_ref[h].astype(jnp.float32).T * enter).astype(jnp.bfloat16)
 
 
 def attend(q_ref, g_ref, state_ref, within_ref, cols_ref, att_ref, sums_ref):
@@ -182,32 +193,27 @@
             at += 1
 
 
-def token_scales(features, sums_ref, tmp_ref):
-    lines = sums_ref.shape[1]
-    tmp_ref[...] = jnp.zeros(tmp_ref.shape, jnp.float32)
-    tmp_ref[0:lines] = jnp.sum(sums_ref[...], axis=0)
-    upright = tmp_ref[...].T
-    half = lines // 2
-    squares = jnp.concatenate([upright[:, i : i + 1] for i in range(half)], axis=0)
-    crossed = jnp.concatenate([upright[:, i : i + 1] for i in range(half, lines)], axis=0)
-    root = jnp.sqrt(squares / features + EPSILON)
-    return 1.0 / root, crossed / (features * root * root)
-
-
 def own_gradient_state(
-    features, q_ref, g_ref, att_ref, sums_ref, cols_ref, ga_ref, pay_ref, scale_ref, tmp_ref
-):
-    heads, tokens, width = q_ref.shape
+    features, decayed_ref, g_ref, att_ref, sums_ref, ga_ref, pay_ref, scale_ref, tmp_ref
+):
+    heads, _, width = g_ref.shape
     per_head = ROW // heads
     depth = width // per_head
-    inverse, factor = token_scales(features, sums_ref, tmp_ref)
-    scale_ref[...] = jnp.broadcast_to(inverse, scale_ref.shape)
+    half = sums_ref.shape[1] // 2
+    sums = jnp.sum(sums_ref[...], axis=0)
+    root = jnp.sqrt(sums[:half] / features + EPSILON)
+    tmp_ref[0:half] = 1.0 / root
+    tmp_ref[half : 2 * half] = sums[half:] / (features * root * root)
+    upright = tmp_ref[...].T
+    shape = scale_ref.shape
+    inverse = jnp.concatenate([upright[:, i : i + 1] for i in range(half)], axis=0)
+    factor = jnp.concatenate([upright[:, i : i + 1] for i in range(half, 2 * half)], axis=0)
+    inverse, factor = jnp.broadcast_to(inverse, shape), jnp.broadcast_to(factor, shape)
+    scale_ref[...] = inverse
     for h in range(heads):
         ga = ((g_ref[h].astype(jnp.float32) - att_ref[h] * factor) * inverse).astype(jnp.bfloat16)
         ga_ref[h] = ga
-        enter = cols_ref[:, heads + h : heads + h + 1]
-        decayed = (q_ref[h].astype(jnp.float32) * enter).astype(jnp.bfloat16)
-        back = dot(decayed, ga, 0, 0)
+        back = dot(decayed_ref[h], ga, 1, 0)
         for part in range(per_head):
             pay_ref[h * per_head + part] = back[part * depth : (part + 1) * depth]
 
@@ -286,12 +292,11 @@
     square = 2 * heads * tokens * tokens * width
     line = 128
 
-    pay, rows, cols = call(
+    pay, rows = call(
         local_states,
         [
             ((ROW, depth + META, width), f32),
             ((line, tokens), f32),
-            ((tokens, line), f32),
         ],
         product,
         [
@@ -308,10 +313,17 @@
         forward_row, [((depth + META, width), f32), ((ROW, META, width), f32)], got.size
     )(got)
     near = passed_along(total, ROW)
-    scores, within = call(
-        within_stretch, [((heads, tokens, tokens), bf16), (block, f32)], 2 * square
-    )(query_rows, key_rows, value_rows, rows, cols)
-    near, scores, within = lax.optimization_barrier((near, scores, within))
+    scores, within, decayed, cols = call(
+        within_stretch,
+        [
+            ((heads, tokens, tokens), bf16),
+            (block, f32),
+            ((heads, width, tokens), bf16),
+            ((tokens, line), f32),
+        ],
+        2 * square,
+    )(query_rows, key_rows, value_rows, rows)
+    near, within = lax.optimization_barrier((near, within))
     (states,) = call(forward_scan, [((ROW, depth, width), f32)], got.size)(got, facts, near)
     state = exchange(states, groups).reshape(heads, width, width)
 
@@ -326,8 +338,8 @@
         functools.partial(own_gradient_state, features),
         [(block, bf16), ((ROW, depth, width), f32), ((tokens, width), f32)],
         product,
-        [pltpu.VMEM((width, width), f32)],
-    )(query_rows, grad_out, attention, sums, cols)
+        [pltpu.VMEM((8, width), f32)],
+    )(decayed, grad_out, attention, sums)
 
     got = exchange(pay, groups)
     (total,) = call(backward_row, [((depth + META, width), f32)], got.size)(got, facts)

time: 95.2 us -> 94.4 us (level)
  no operation moved by 1% of the time
where the time goes in v3:
time: 94.4 us; the launch traced here: 94 us
  blocking collectives  72.1 us (76%)
  starting transfers between devices  9.34 us (10%)
  Pallas kernels  7.02 us (7%)
  waiting for transfers between devices  4.7 us (5%)
    all_to_all x4, blocking collectives, exchange(): lax.all_to_all(block, 'seq', split_axis=0, concat_axis=0, tiled=True, axi...  62.7 us
    all_to_all x1, blocking collectives, per_device(): sums = lax.all_to_all(sums, 'head', split_axis=0, concat_axis=0, tiled=True)  9.46 us
    ppermute x2, starting transfers between devices, passed_along(): return lax.ppermute(block, 'seq', route)  9.34 us
    pallas_call x10, Pallas kernels, run(): pl.pallas_call(body, out_shape=shapes, in_specs=[pl.BlockSpec(memory_spac...  7.02 us
    ppermute x2, waiting for transfers between devices, passed_along(): return lax.ppermute(block, 'seq', route)  4.7 us
  transfers between devices with their start and end apart: 2, of which 2 were waited for; matrix products, arithmetic and copies ran while one was open for 0% of the time, Pallas kernels for 3%

profile of v3, /device:TPU:136, one launch (start us, length us, event | category | flops | bytes accessed | tf_op | source)
XLA Modules:
  0.0 94.0 jit_solution(9456794576996907514)
XLA Ops:
  0.6 2.0 %local_states.1 = (f32[16,40,128]{2,1,0:T(8,128)S(1)}, f32[128,256]{1,0:T(8,128)S(1)}) custom-call(f32[4,256]{1,0:T(4,128)} %gate_hbm.1, s32[1,256]{1,0:T(1,128)} %bitcast.6, bf16[4,256,128]{2,1,0:T(8,128)(2,1)} %k_ref.5, bf16[4,256,128]{2,1,0:T(8,128)(2,1)} %v_ref.5), custom_call_target="tpu_custom_call" | custom-call | flops 33554432 | bytes 988160 | tf_op jit(solution)/shard_map/local_states/pallas_call | solution.py:27
  2.7 0.0 copy-start.1
  2.7 0.0 copy-start.2
  2.7 20.6 %all_to_all.25.got_ref = f32[16,40,128]{2,1,0:T(8,128)S(1)} all-to-all(f32[16,40,128]{2,1,0:T(8,128)S(1)} %get-tuple-element.30), channel_id=1, replica_groups={{0,8,16,24,32,40,48,56,64,72,80,88,96,104,112,120},{128,136,144,152,160..., dimensions={0} | all-to-all | bytes 655360 | tf_op jit(solution)/shard_map/all_to_all | solution.py:273
  23.3 0.0 copy-start
  23.3 7.4 %collective-permute-start = (f32[40,128]{1,0:T(8,128)S(1)}, f32[40,128]{1,0:T(8,128)S(1)}, u32[]{:S(2)}, u32[]{:S(2)}) collective-permute-start(f32[40,128]{1,0:T(8,128)S(1)} %get-tuple-element.32), channel_id=1, source_target_pairs={{0,128},{8,136},{16,144},{24,152},{32,160},{40,168},{48,176},{56,1... | collective-permute-start | bytes 61448 | tf_op jit(solution)/shard_map/ppermute | solution.py:281
  30.8 0.0 copy-done.1
  30.8 0.0 copy-done.2
  30.8 0.0 copy-done
  30.8 0.7 within_stretch.1
  31.5 0.7 collective-permute-done.near_ref
  32.3 0.0 copy-start.3
  32.3 14.1 %all_to_all.26 = f32[16,32,128]{2,1,0:T(8,128)S(1)} all-to-all(f32[16,32,128]{2,1,0:T(8,128)S(1)} %forward_scan.1), channel_id=1, replica_groups={{0,8,16,24,32,40,48,56,64,72,80,88,96,104,112,120},{128,136,144,152,160..., dimensions={0} | all-to-all | bytes 524288 | tf_op jit(solution)/shard_map/all_to_all | solution.py:273
  46.4 0.0 copy-done.3
  46.4 0.4 attend.1
  46.8 9.5 %all_to_all.27.sums_ref = f32[8,4,128]{2,1,0:T(4,128)S(1)} all-to-all(f32[8,4,128]{2,1,0:T(4,128)S(1)} %get-tuple-element.38), channel_id=1, replica_groups=mesh['seq'=128,'head'=8] {'head'}, dimensions={0} | all-to-all | bytes 32768 | tf_op jit(solution)/shard_map/all_to_all | solution.py:335
  56.3 0.5 own_gradient_state.1
  56.8 14.4 %all_to_all.28.got_ref = f32[16,32,128]{2,1,0:T(8,128)S(1)} all-to-all(f32[16,32,128]{2,1,0:T(8,128)S(1)} %get-tuple-element.44), channel_id=1, replica_groups={{0,8,16,24,32,40,48,56,64,72,80,88,96,104,112,120},{128,136,144,152,160..., dimensions={0} | all-to-all | bytes 524288 | tf_op jit(solution)/shard_map/all_to_all | solution.py:273
  71.3 1.9 %collective-permute-start.1 = (f32[40,128]{1,0:T(8,128)S(1)}, f32[40,128]{1,0:T(8,128)S(1)}, u32[]{:S(2)}, u32[]{:S(2)}) collective-permute-start(f32[40,128]{1,0:T(8,128)S(1)} %backward_row.1), channel_id=1, source_target_pairs={{128,0},{136,8},{144,16},{152,24},{160,32},{168,40},{176,48},{184,... | collective-permute-start | bytes 61448 | tf_op jit(solution)/shard_map/ppermute | solution.py:281
  73.2 2.1 %inner_gradients.1 = (bf16[4,256,128]{2,1,0:T(8,128)(2,1)}, bf16[4,256,128]{2,1,0:T(8,128)(2,1)}, f32[4,256,128]{2,1,0:T(8,128)S(1)}, f32[4,256,128]{2,1,0:T(8,128)S(1)}) custom-call(bf16[4,256,128]{2,1,0:T(8,128)(2,1)S(1)} %copy-done.2, bf16[4,256,128]{2,1,0:T(8,128)(2,1)S(1)} %copy-done, bf16[4,256,128]{2,1,0:T(8,128)(2,1)S(1)} %copy-done.1, ...), custom_call_target="tpu_custom_call" | custom-call | flops 301989888 | bytes 4325376 | tf_op jit(solution)/shard_map/inner_gradients/pallas_call | solution.py:27
  75.3 4.0 %collective-permute-done.1.near_ref = f32[40,128]{1,0:T(8,128)S(1)} collective-permute-done((f32[40,128]{1,0:T(8,128)S(1)}, f32[40,128]{1,0:T(8,128)S(1)}, u32[]{:S(2)}, u32[]{:S(2)}) %collective-permute-start.1) | collective-permute-done | bytes 20512 | tf_op jit(solution)/shard_map/ppermute | solution.py:281
  79.4 13.6 %all_to_all.29 = f32[16,32,128]{2,1,0:T(8,128)S(1)} all-to-all(f32[16,32,128]{2,1,0:T(8,128)S(1)} %backward_scan.1), channel_id=1, replica_groups={{0,8,16,24,32,40,48,56,64,72,80,88,96,104,112,120},{128,136,144,152,160..., dimensions={0} | all-to-all | bytes 524288 | tf_op jit(solution)/shard_map/all_to_all | solution.py:273
  92.9 1.0 %outer_gradients.1 = (bf16[4,256,128]{2,1,0:T(8,128)(2,1)}, bf16[4,256,128]{2,1,0:T(8,128)(2,1)}) custom-call(bf16[4,256,128]{2,1,0:T(8,128)(2,1)S(1)} %copy-done, bf16[4,256,128]{2,1,0:T(8,128)(2,1)S(1)} %copy-done.1, f32[4,256,128]{2,1,0:T(8,128)S(1)} %get-tuple-element.47.ki_ref, f32[4,256,128]{2,1,0:T(8,128)S(1)} %get-tuple-element.48.vi_ref, ...), custom_call_target="tpu_custom_call" | custom-call | flops 67108864 | bytes 2490368 | tf_op jit(solution)/shard_map/outer_gradients/pallas_call | solution.py:27
  (4 shorter events, 0.2 us)
Async XLA Ops:
  2.7 28.1 %copy-start.1 = (bf16[4,256,128]{2,1,0:T(8,128)(2,1)S(1)}, bf16[4,256,128]{2,1,0:T(8,128)(2,1)}, u32[]{:S(2)}) copy-start(bf16[4,256,128]{2,1,0:T(8,128)(2,1)} %v_ref.5) | copy-start | bytes 786436
  2.7 28.1 %copy-start.2 = (bf16[4,256,128]{2,1,0:T(8,128)(2,1)S(1)}, bf16[4,256,128]{2,1,0:T(8,128)(2,1)}, u32[]{:S(2)}) copy-start(bf16[4,256,128]{2,1,0:T(8,128)(2,1)} %q_ref.5) | copy-start | bytes 786436
  23.3 7.5 %copy-start = (bf16[4,256,128]{2,1,0:T(8,128)(2,1)S(1)}, bf16[4,256,128]{2,1,0:T(8,128)(2,1)}, u32[]{:S(2)}) copy-start(bf16[4,256,128]{2,1,0:T(8,128)(2,1)} %k_ref.5) | copy-start | bytes 786436
  23.3 8.9 %collective-permute-start = (f32[40,128]{1,0:T(8,128)S(1)}, f32[40,128]{1,0:T(8,128)S(1)}, u32[]{:S(2)}, u32[]{:S(2)}) collective-permute-start(f32[40,128]{1,0:T(8,128)S(1)} %get-tuple-element.32), channel_id=1, source_target_pairs={{0,128},{8,136},{16,144},{24,152},{32,160},{40,168},{48,176},{56,1... | collective-permute-start | bytes 61448 | tf_op jit(solution)/shard_map/ppermute | solution.py:281
  32.3 14.1 %copy-start.3 = (bf16[4,256,128]{2,1,0:T(8,128)(2,1)S(1)}, bf16[4,256,128]{2,1,0:T(8,128)(2,1)}, u32[]{:S(2)}) copy-start(bf16[4,256,128]{2,1,0:T(8,128)(2,1)} %g_ref.3) | copy-start | bytes 786436
  71.3 8.0 %collective-permute-start.1 = (f32[40,128]{1,0:T(8,128)S(1)}, f32[40,128]{1,0:T(8,128)S(1)}, u32[]{:S(2)}, u32[]{:S(2)}) collective-permute-start(f32[40,128]{1,0:T(8,128)S(1)} %backward_row.1), channel_id=1, source_target_pairs={{128,0},{136,8},{144,16},{152,24},{160,32},{168,40},{176,48},{184,... | collective-permute-start | bytes 61448 | tf_op jit(solution)/shard_map/ppermute | solution.py:281

commit v4 on v3

--- a/solution.py
+++ b/solution.py
@@ -81,10 +81,10 @@
     rows_ref[3 * heads : 3 * heads + 1] = ep.astype(jnp.float32)
     fact = lax.broadcasted_iota(jnp.int32, (META, width), 0)
     first_f, last_f = first.astype(jnp.float32), last.astype(jnp.float32)
-    for h in range(heads):
-        keys[h].wait()
+    for copy in (*keys, *values):
+        copy.wait()
+    for h in range(heads):
         decayed = (k_ref[h].T.astype(jnp.float32) * leave[h : h + 1]).astype(jnp.bfloat16)
-        values[h].wait()
         state = dot(decayed, v_ref[h], 1, 0)
         facts = jnp.where(
             fact == 0,

time: 94.4 us -> 93.8 us (level)
  no operation moved by 1% of the time
where the time goes in v4:
time: 93.8 us; the launch traced here: 93.4 us
  blocking collectives  72.2 us (77%)
  starting transfers between devices  9.35 us (10%)
  Pallas kernels  6.48 us (7%)
  waiting for transfers between devices  4.61 us (5%)
    all_to_all x4, blocking collectives, exchange(): lax.all_to_all(block, 'seq', split_axis=0, concat_axis=0, tiled=True, axi...  62.8 us
    all_to_all x1, blocking collectives, per_device(): sums = lax.all_to_all(sums, 'head', split_axis=0, concat_axis=0, tiled=True)  9.46 us
    ppermute x2, starting transfers between devices, passed_along(): return lax.ppermute(block, 'seq', route)  9.35 us
    pallas_call x10, Pallas kernels, run(): pl.pallas_call(body, out_shape=shapes, in_specs=[pl.BlockSpec(memory_spac...  6.48 us
    ppermute x2, waiting for transfers between devices, passed_along(): return lax.ppermute(block, 'seq', route)  4.61 us
  transfers between devices with their start and end apart: 2, of which 2 were waited for; matrix products, arithmetic and copies ran while one was open for 0% of the time, Pallas kernels for 3%

profile of v4, /device:TPU:136, one launch (start us, length us, event | category | flops | bytes accessed | tf_op | source)
XLA Modules:
  0.0 93.4 jit_solution(15982336655336801577)
XLA Ops:
  0.6 1.5 %local_states.1 = (f32[16,40,128]{2,1,0:T(8,128)S(1)}, f32[128,256]{1,0:T(8,128)S(1)}) custom-call(f32[4,256]{1,0:T(4,128)} %gate_hbm.1, s32[1,256]{1,0:T(1,128)} %bitcast.6, bf16[4,256,128]{2,1,0:T(8,128)(2,1)} %k_ref.5, bf16[4,256,128]{2,1,0:T(8,128)(2,1)} %v_ref.5), custom_call_target="tpu_custom_call" | custom-call | flops 33554432 | bytes 988160 | tf_op jit(solution)/shard_map/local_states/pallas_call | solution.py:27
  2.1 0.0 copy-start.1
  2.1 0.0 copy-start.2
  2.1 20.6 %all_to_all.25.got_ref = f32[16,40,128]{2,1,0:T(8,128)S(1)} all-to-all(f32[16,40,128]{2,1,0:T(8,128)S(1)} %get-tuple-element.30), channel_id=1, replica_groups={{0,8,16,24,32,40,48,56,64,72,80,88,96,104,112,120},{128,136,144,152,160..., dimensions={0} | all-to-all | bytes 655360 | tf_op jit(solution)/shard_map/all_to_all | solution.py:273
  22.8 0.0 copy-start
  22.8 7.4 %collective-permute-start = (f32[40,128]{1,0:T(8,128)S(1)}, f32[40,128]{1,0:T(8,128)S(1)}, u32[]{:S(2)}, u32[]{:S(2)}) collective-permute-start(f32[40,128]{1,0:T(8,128)S(1)} %get-tuple-element.32), channel_id=1, source_target_pairs={{0,128},{8,136},{16,144},{24,152},{32,160},{40,168},{48,176},{56,1... | collective-permute-start | bytes 61448 | tf_op jit(solution)/shard_map/ppermute | solution.py:281
  30.2 0.0 copy-done.1
  30.3 0.0 copy-done.2
  30.3 0.0 copy-done
  30.3 0.7 within_stretch.1
  31.0 0.7 collective-permute-done.near_ref
  31.8 0.0 copy-start.3
  31.8 14.1 %all_to_all.26 = f32[16,32,128]{2,1,0:T(8,128)S(1)} all-to-all(f32[16,32,128]{2,1,0:T(8,128)S(1)} %forward_scan.1), channel_id=1, replica_groups={{0,8,16,24,32,40,48,56,64,72,80,88,96,104,112,120},{128,136,144,152,160..., dimensions={0} | all-to-all | bytes 524288 | tf_op jit(solution)/shard_map/all_to_all | solution.py:273
  45.9 0.0 copy-done.3
  45.9 0.4 attend.1
  46.3 9.5 %all_to_all.27.sums_ref = f32[8,4,128]{2,1,0:T(4,128)S(1)} all-to-all(f32[8,4,128]{2,1,0:T(4,128)S(1)} %get-tuple-element.38), channel_id=1, replica_groups=mesh['seq'=128,'head'=8] {'head'}, dimensions={0} | all-to-all | bytes 32768 | tf_op jit(solution)/shard_map/all_to_all | solution.py:335
  55.8 0.5 own_gradient_state.1
  56.3 14.4 %all_to_all.28.got_ref = f32[16,32,128]{2,1,0:T(8,128)S(1)} all-to-all(f32[16,32,128]{2,1,0:T(8,128)S(1)} %get-tuple-element.44), channel_id=1, replica_groups={{0,8,16,24,32,40,48,56,64,72,80,88,96,104,112,120},{128,136,144,152,160..., dimensions={0} | all-to-all | bytes 524288 | tf_op jit(solution)/shard_map/all_to_all | solution.py:273
  70.7 1.9 %collective-permute-start.1 = (f32[40,128]{1,0:T(8,128)S(1)}, f32[40,128]{1,0:T(8,128)S(1)}, u32[]{:S(2)}, u32[]{:S(2)}) collective-permute-start(f32[40,128]{1,0:T(8,128)S(1)} %backward_row.1), channel_id=1, source_target_pairs={{128,0},{136,8},{144,16},{152,24},{160,32},{168,40},{176,48},{184,... | collective-permute-start | bytes 61448 | tf_op jit(solution)/shard_map/ppermute | solution.py:281
  72.7 2.1 %inner_gradients.1 = (bf16[4,256,128]{2,1,0:T(8,128)(2,1)}, bf16[4,256,128]{2,1,0:T(8,128)(2,1)}, f32[4,256,128]{2,1,0:T(8,128)S(1)}, f32[4,256,128]{2,1,0:T(8,128)S(1)}) custom-call(bf16[4,256,128]{2,1,0:T(8,128)(2,1)S(1)} %copy-done.2, bf16[4,256,128]{2,1,0:T(8,128)(2,1)S(1)} %copy-done, bf16[4,256,128]{2,1,0:T(8,128)(2,1)S(1)} %copy-done.1, ...), custom_call_target="tpu_custom_call" | custom-call | flops 301989888 | bytes 4325376 | tf_op jit(solution)/shard_map/inner_gradients/pallas_call | solution.py:27
  74.8 3.9 %collective-permute-done.1.near_ref = f32[40,128]{1,0:T(8,128)S(1)} collective-permute-done((f32[40,128]{1,0:T(8,128)S(1)}, f32[40,128]{1,0:T(8,128)S(1)}, u32[]{:S(2)}, u32[]{:S(2)}) %collective-permute-start.1) | collective-permute-done | bytes 20512 | tf_op jit(solution)/shard_map/ppermute | solution.py:281
  78.7 13.6 %all_to_all.29 = f32[16,32,128]{2,1,0:T(8,128)S(1)} all-to-all(f32[16,32,128]{2,1,0:T(8,128)S(1)} %backward_scan.1), channel_id=1, replica_groups={{0,8,16,24,32,40,48,56,64,72,80,88,96,104,112,120},{128,136,144,152,160..., dimensions={0} | all-to-all | bytes 524288 | tf_op jit(solution)/shard_map/all_to_all | solution.py:273
  92.4 1.0 %outer_gradients.1 = (bf16[4,256,128]{2,1,0:T(8,128)(2,1)}, bf16[4,256,128]{2,1,0:T(8,128)(2,1)}) custom-call(bf16[4,256,128]{2,1,0:T(8,128)(2,1)S(1)} %copy-done, bf16[4,256,128]{2,1,0:T(8,128)(2,1)S(1)} %copy-done.1, f32[4,256,128]{2,1,0:T(8,128)S(1)} %get-tuple-element.47.ki_ref, f32[4,256,128]{2,1,0:T(8,128)S(1)} %get-tuple-element.48.vi_ref, ...), custom_call_target="tpu_custom_call" | custom-call | flops 67108864 | bytes 2490368 | tf_op jit(solution)/shard_map/outer_gradients/pallas_call | solution.py:27
  (4 shorter events, 0.2 us)
Async XLA Ops:
  2.1 28.1 %copy-start.1 = (bf16[4,256,128]{2,1,0:T(8,128)(2,1)S(1)}, bf16[4,256,128]{2,1,0:T(8,128)(2,1)}, u32[]{:S(2)}) copy-start(bf16[4,256,128]{2,1,0:T(8,128)(2,1)} %v_ref.5) | copy-start | bytes 786436
  2.1 28.1 %copy-start.2 = (bf16[4,256,128]{2,1,0:T(8,128)(2,1)S(1)}, bf16[4,256,128]{2,1,0:T(8,128)(2,1)}, u32[]{:S(2)}) copy-start(bf16[4,256,128]{2,1,0:T(8,128)(2,1)} %q_ref.5) | copy-start | bytes 786436
  22.8 7.5 %copy-start = (bf16[4,256,128]{2,1,0:T(8,128)(2,1)S(1)}, bf16[4,256,128]{2,1,0:T(8,128)(2,1)}, u32[]{:S(2)}) copy-start(bf16[4,256,128]{2,1,0:T(8,128)(2,1)} %k_ref.5) | copy-start | bytes 786436
  22.8 8.9 %collective-permute-start = (f32[40,128]{1,0:T(8,128)S(1)}, f32[40,128]{1,0:T(8,128)S(1)}, u32[]{:S(2)}, u32[]{:S(2)}) collective-permute-start(f32[40,128]{1,0:T(8,128)S(1)} %get-tuple-element.32), channel_id=1, source_target_pairs={{0,128},{8,136},{16,144},{24,152},{32,160},{40,168},{48,176},{56,1... | collective-permute-start | bytes 61448 | tf_op jit(solution)/shard_map/ppermute | solution.py:281
  31.8 14.1 %copy-start.3 = (bf16[4,256,128]{2,1,0:T(8,128)(2,1)S(1)}, bf16[4,256,128]{2,1,0:T(8,128)(2,1)}, u32[]{:S(2)}) copy-start(bf16[4,256,128]{2,1,0:T(8,128)(2,1)} %g_ref.3) | copy-start | bytes 786436
  70.7 7.9 %collective-permute-start.1 = (f32[40,128]{1,0:T(8,128)S(1)}, f32[40,128]{1,0:T(8,128)S(1)}, u32[]{:S(2)}, u32[]{:S(2)}) collective-permute-start(f32[40,128]{1,0:T(8,128)S(1)} %backward_row.1), channel_id=1, source_target_pairs={{128,0},{136,8},{144,16},{152,24},{160,32},{168,40},{176,48},{184,... | collective-permute-start | bytes 61448 | tf_op jit(solution)/shard_map/ppermute | solution.py:281

commit v5 on v4

--- a/solution.py
+++ b/solution.py
@@ -9,6 +9,7 @@
 
 EPSILON = 1e-06
 ROW = 16
+LEAD = 4
 META = 8
 HIGH = lax.Precision.HIGHEST
 
@@ -17,6 +18,11 @@
     return lax.dot_general(
         a, b, (((da,), (db,)), ((), ())), preferred_element_type=jnp.float32
     )
+
+
+def listed():
+    lead = jnp.where(lax.axis_index("seq") < ROW, 0, LEAD)
+    return lambda member: lax.rem(member + ROW - lead, ROW)
 
 
 def call(body, outs, flops, scratch=(), from_hbm=False, to_hbm=False):
@@ -53,6 +59,7 @@
     width = k_ref.shape[2]
     per_head = ROW // heads
     depth = width // per_head
+    slot = listed()
     gates = pltpu.make_async_copy(gate_hbm, gate_ref, sems.at[0])
     ids = pltpu.make_async_copy(ep_hbm, ep_ref, sems.at[1])
     gates.start()
@@ -79,7 +86,7 @@
     rows_ref[heads : 2 * heads] = jnp.where(ep == first, jnp.exp(run), 0.0)
     rows_ref[2 * heads : 3 * heads] = leave
     rows_ref[3 * heads : 3 * heads + 1] = ep.astype(jnp.float32)
-    fact = lax.broadcasted_iota(jnp.int32, (META, width), 0)
+    fact = lax.broadcasted_iota(jnp.int32, (1, width), 1)
     first_f, last_f = first.astype(jnp.float32), last.astype(jnp.float32)
     for copy in (*keys, *values):
         copy.wait()
@@ -92,9 +99,9 @@
             jnp.where(fact == 1, first_f, jnp.where(fact == 2, last_f, 0.0)),
         )
         for part in range(per_head):
-            p = h * per_head + part
-            pay_ref[p, 0:depth] = state[part * depth : (part + 1) * depth]
-            pay_ref[p, depth : depth + META] = facts
+            at = slot(h * per_head + part) * (depth + 1)
+            pay_ref[pl.ds(at, depth)] = state[part * depth : (part + 1) * depth]
+            pay_ref[pl.ds(at + depth, 1)] = facts
 
 
 def facts_of(fact_ref, j):
@@ -109,44 +116,59 @@
 
 
 def forward_row(got_ref, sum_ref, fact_ref):
-    depth = got_ref.shape[1] - META
+    stride = got_ref.shape[0] // ROW
+    depth, shape = stride - 1, (1, got_ref.shape[1])
+    slot = listed()
     for j in range(ROW):
-        fact_ref[j] = got_ref[j, depth : depth + META]
-    state, mark = got_ref[0, 0:depth], facts_of(fact_ref, 0)[2]
+        facts = got_ref[pl.ds(slot(j) * stride + depth, 1)]
+        for i in range(3):
+            fact_ref[j, i : i + 1] = jnp.broadcast_to(facts[:, i : i + 1], shape)
+    state, mark = got_ref[pl.ds(slot(0) * stride, depth)], facts_of(fact_ref, 0)[2]
     for j in range(1, ROW):
         decay, _, last = facts_of(fact_ref, j)
-        state = jnp.where(mark == last, jnp.exp(decay), 0.0) * state + got_ref[j, 0:depth]
+        kept = jnp.where(mark == last, jnp.exp(decay), 0.0)
+        state = kept * state + got_ref[pl.ds(slot(j) * stride, depth)]
         mark = last
     summary(sum_ref, state, mark)
 
 
 def backward_row(got_ref, fact_ref, sum_ref):
-    state, mark = got_ref[ROW - 1], facts_of(fact_ref, ROW - 1)[1]
+    slot = listed()
+    state, mark = got_ref[slot(ROW - 1)], facts_of(fact_ref, ROW - 1)[1]
     for j in range(ROW - 2, -1, -1):
         decay, first, _ = facts_of(fact_ref, j)
-        state = jnp.where(mark == first, jnp.exp(decay), 0.0) * state + got_ref[j]
+        state = jnp.where(mark == first, jnp.exp(decay), 0.0) * state + got_ref[slot(j)]
         mark = first
     summary(sum_ref, state, mark)
 
 
 def forward_scan(got_ref, fact_ref, near_ref, out_ref):
     depth = out_ref.shape[1]
+    slot = listed()
     state, mark = near_ref[0:depth], near_ref[depth + 1 : depth + 2]
     for j in range(ROW):
         decay, first, last = facts_of(fact_ref, j)
-        out_ref[j] = jnp.where(mark == first, state, 0.0)
-        state = jnp.where(mark == last, jnp.exp(decay), 0.0) * state + got_ref[j, 0:depth]
+        out_ref[slot(j)] = jnp.where(mark == first, state, 0.0)
+        kept = jnp.where(mark == last, jnp.exp(decay), 0.0)
+        state = kept * state + got_ref[pl.ds(slot(j) * (depth + 1), depth)]
         mark = last
 
 
 def backward_scan(got_ref, fact_ref, near_ref, out_ref):
     depth = out_ref.shape[1]
+    slot = listed()
     state, mark = near_ref[0:depth], near_ref[depth + 1 : depth + 2]
     for j in range(ROW - 1, -1, -1):
         decay, first, last = facts_of(fact_ref, j)
-        out_ref[j] = jnp.where(mark == last, state, 0.0)
-        state = jnp.where(mark == first, jnp.exp(decay), 0.0) * state + got_ref[j]
+        out_ref[slot(j)] = jnp.where(mark == last, state, 0.0)
+        state = jnp.where(mark == first, jnp.exp(decay), 0.0) * state + got_ref[slot(j)]
         mark = first
+
+
+def head_state(state_ref, slot, heads, h):
+    per_head = ROW // heads
+    slices = [state_ref[slot(h * per_head + part)] for part in range(per_head)]
+    return jnp.concatenate(slices, axis=0).astype(jnp.bfloat16)
 
 
 def decays_of(rows_ref, cols_ref, heads, h):
@@ -175,9 +197,10 @@
 
 def attend(q_ref, g_ref, state_ref, within_ref, cols_ref, att_ref, sums_ref):
     heads, tokens, width = q_ref.shape
+    slot = listed()
     squares = crossed = jnp.zeros((tokens, width), jnp.float32)
     for h in range(heads):
-        state = state_ref[h].astype(jnp.bfloat16)
+        state = head_state(state_ref, slot, heads, h)
         enter = cols_ref[:, heads + h : heads + h + 1]
         att = within_ref[h] + dot(q_ref[h], state, 1, 0) * enter
         att_ref[h] = att
@@ -199,6 +222,7 @@
     heads, _, width = g_ref.shape
     per_head = ROW // heads
     depth = width // per_head
+    slot = listed()
     half = sums_ref.shape[1] // 2
     sums = jnp.sum(sums_ref[...], axis=0)
     root = jnp.sqrt(sums[:half] / features + EPSILON)
@@ -215,7 +239,7 @@
         ga_ref[h] = ga
         back = dot(decayed_ref[h], ga, 1, 0)
         for part in range(per_head):
-            pay_ref[h * per_head + part] = back[part * depth : (part + 1) * depth]
+            pay_ref[slot(h * per_head + part)] = back[part * depth : (part + 1) * depth]
 
 
 def inner_gradients(
@@ -235,13 +259,14 @@
     vi_ref,
 ):
     heads = q_ref.shape[0]
+    slot = listed()
     for h in range(heads):
         norm_ref[h] = (att_ref[h] * scale_ref[...]).astype(jnp.bfloat16)
         ga = ga_ref[h]
         decays = decays_of(rows_ref, cols_ref, heads, h)
         slope = (dot(ga, v_ref[h], 1, 1) * decays).astype(jnp.bfloat16)
         enter = cols_ref[:, heads + h : heads + h + 1]
-        state = state_ref[h].astype(jnp.bfloat16)
+        state = head_state(state_ref, slot, heads, h)
         gq_ref[h] = (dot(slope, k_ref[h], 1, 0) + dot(ga, state, 1, 1) * enter).astype(jnp.bfloat16)
         ki_ref[h] = dot(slope, q_ref[h], 0, 0)
         vi_ref[h] = dot(scores_ref[h], ga, 0, 0)
@@ -251,9 +276,10 @@
     k_ref, v_ref, ki_ref, vi_ref, back_ref, cols_ref, gk_hbm, gv_hbm, gk_ref, gv_ref, sems
 ):
     heads = k_ref.shape[0]
+    slot = listed()
     copies = []
     for h in range(heads):
-        back = back_ref[h].astype(jnp.bfloat16)
+        back = head_state(back_ref, slot, heads, h)
         leave = cols_ref[:, 2 * heads + h : 2 * heads + h + 1]
         gk_ref[h] = (ki_ref[h] + dot(v_ref[h], back, 1, 1) * leave).astype(jnp.bfloat16)
         copies.append(pltpu.make_async_copy(gk_ref.at[h], gk_hbm.at[h], sems.at[2 * h]))
@@ -285,7 +311,9 @@
     heads, tokens, width = query_rows.shape
     depth = heads * width // ROW
     devices = lax.axis_size("seq")
-    groups = [list(range(at, at + ROW)) for at in range(0, devices, ROW)]
+    groups = [
+        [at + (i + (LEAD if at else 0)) % ROW for i in range(ROW)] for at in range(0, devices, ROW)
+    ]
     f32, bf16 = jnp.float32, jnp.bfloat16
     block = (heads, tokens, width)
     product = 2 * heads * tokens * width * width
@@ -295,7 +323,7 @@
     pay, rows = call(
         local_states,
         [
-            ((ROW, depth + META, width), f32),
+            ((ROW * (depth + 1), width), f32),
             ((line, tokens), f32),
         ],
         product,
@@ -308,7 +336,8 @@
         ],
         from_hbm=True,
     )(*map(in_hbm, (log_gate, episode.reshape(1, tokens), key_rows, value_rows)))
-    got = exchange(pay, groups)
+    dense = (ROW, depth + 1, 1, width)
+    got = exchange(pay.reshape(dense), groups).reshape(pay.shape)
     total, facts = call(
         forward_row, [((depth + META, width), f32), ((ROW, META, width), f32)], got.size
     )(got)
@@ -325,7 +354,7 @@
     )(query_rows, key_rows, value_rows, rows)
     near, within = lax.optimization_barrier((near, within))
     (states,) = call(forward_scan, [((ROW, depth, width), f32)], got.size)(got, facts, near)
-    state = exchange(states, groups).reshape(heads, width, width)
+    state = exchange(states, groups)
 
     lines = 2 * tokens // width
     across = lax.axis_size("head")
@@ -362,7 +391,7 @@
     )
     near, key_inner, value_inner = lax.optimization_barrier((near, key_inner, value_inner))
     (states,) = call(backward_scan, [((ROW, depth, width), f32)], got.size)(got, facts, near)
-    back = exchange(states, groups).reshape(heads, width, width)
+    back = exchange(states, groups)
     key_grad, value_grad = call(
         outer_gradients,
         [(block, bf16), (block, bf16)],

time: 93.8 us -> 90.6 us (0.966)
  the two profiles are of different devices: /device:TPU:136 before, /device:TPU:8 now
where the time goes in v5:
time: 90.6 us; the launch traced here: 90.2 us
  blocking collectives  75.8 us (84%)
  Pallas kernels  6.66 us (7%)
  waiting for transfers between devices  4.31 us (5%)
  starting transfers between devices  2.58 us (3%)
    all_to_all x4, blocking collectives, exchange(): lax.all_to_all(block, 'seq', split_axis=0, concat_axis=0, tiled=True, axi...  67.2 us
    all_to_all x1, blocking collectives, per_device(): sums = lax.all_to_all(sums, 'head', split_axis=0, concat_axis=0, tiled=True)  8.62 us
    pallas_call x10, Pallas kernels, run(): pl.pallas_call(body, out_shape=shapes, in_specs=[pl.BlockSpec(memory_spac...  6.66 us
    ppermute x2, waiting for transfers between devices, passed_along(): return lax.ppermute(block, 'seq', route)  4.31 us
    ppermute x2, starting transfers between devices, passed_along(): return lax.ppermute(block, 'seq', route)  2.58 us
  transfers between devices with their start and end apart: 2, of which 2 were waited for; matrix products, arithmetic and copies ran while one was open for 0% of the time, Pallas kernels for 3%

profile of v5, /device:TPU:8, one launch (start us, length us, event | category | flops | bytes accessed | tf_op | source)
XLA Modules:
  0.0 90.2 jit_solution(1707098018793190359)
XLA Ops:
  0.6 1.5 %local_states.1 = (f32[528,128]{1,0:T(8,128)S(1)}, f32[128,256]{1,0:T(8,128)S(1)}) custom-call(f32[4,256]{1,0:T(4,128)} %gate_hbm.1, s32[1,256]{1,0:T(1,128)} %bitcast.6, bf16[4,256,128]{2,1,0:T(8,128)(2,1)} %k_ref.5, bf16[4,256,128]{2,1,0:T(8,128)(2,1)} %v_ref.5), custom_call_target="tpu_custom_call" | custom-call | flops 33554432 | bytes 930816 | tf_op jit(solution)/shard_map/local_states/pallas_call | solution.py:33
  2.1 0.0 copy-start.1
  2.1 0.0 copy-start.2
  2.1 23.9 %all_to_all.25 = f32[16,33,1,128]{3,2,1,0:T(1,128)S(1)} all-to-all(f32[16,33,1,128]{3,2,1,0:T(1,128)S(1)} %bitcast.5), channel_id=1, replica_groups={{0,8,16,24,32,40,48,56,64,72,80,88,96,104,112,120},{160,168,176,184,192..., dimensions={0} | all-to-all | bytes 540672 | tf_op jit(solution)/shard_map/all_to_all | solution.py:299
  26.0 0.0 copy-start
  26.1 0.2 forward_row.1
  26.2 1.3 %collective-permute-start = (f32[40,128]{1,0:T(8,128)S(1)}, f32[40,128]{1,0:T(8,128)S(1)}, u32[]{:S(2)}, u32[]{:S(2)}) collective-permute-start(f32[40,128]{1,0:T(8,128)S(1)} %get-tuple-element.32), channel_id=1, source_target_pairs={{0,128},{8,136},{16,144},{24,152},{32,160},{40,168},{48,176},{56,1... | collective-permute-start | bytes 61448 | tf_op jit(solution)/shard_map/ppermute | solution.py:307
  27.5 0.0 copy-done.1
  27.5 0.0 copy-done.2
  27.5 0.0 copy-done
  27.5 0.7 within_stretch.1
  28.3 0.7 collective-permute-done.near_ref
  29.0 0.1 forward_scan.1
  29.0 0.0 copy-start.3
  29.1 13.2 %all_to_all.26.state_ref = f32[16,32,128]{2,1,0:T(8,128)S(1)} all-to-all(f32[16,32,128]{2,1,0:T(8,128)S(1)} %forward_scan.1), channel_id=1, replica_groups={{0,8,16,24,32,40,48,56,64,72,80,88,96,104,112,120},{160,168,176,184,192..., dimensions={0} | all-to-all | bytes 524288 | tf_op jit(solution)/shard_map/all_to_all | solution.py:299
  42.3 0.0 copy-done.3
  42.3 0.4 attend.1
  42.7 8.6 %all_to_all.27.sums_ref = f32[8,4,128]{2,1,0:T(4,128)S(1)} all-to-all(f32[8,4,128]{2,1,0:T(4,128)S(1)} %get-tuple-element.38), channel_id=1, replica_groups=mesh['seq'=128,'head'=8] {'head'}, dimensions={0} | all-to-all | bytes 32768 | tf_op jit(solution)/shard_map/all_to_all | solution.py:364
  51.3 0.5 own_gradient_state.1
  51.9 14.9 %all_to_all.28.got_ref = f32[16,32,128]{2,1,0:T(8,128)S(1)} all-to-all(f32[16,32,128]{2,1,0:T(8,128)S(1)} %get-tuple-element.44), channel_id=1, replica_groups={{0,8,16,24,32,40,48,56,64,72,80,88,96,104,112,120},{160,168,176,184,192..., dimensions={0} | all-to-all | bytes 524288 | tf_op jit(solution)/shard_map/all_to_all | solution.py:299
  66.9 1.3 %collective-permute-start.1 = (f32[40,128]{1,0:T(8,128)S(1)}, f32[40,128]{1,0:T(8,128)S(1)}, u32[]{:S(2)}, u32[]{:S(2)}) collective-permute-start(f32[40,128]{1,0:T(8,128)S(1)} %backward_row.1), channel_id=1, source_target_pairs={{128,0},{136,8},{144,16},{152,24},{160,32},{168,40},{176,48},{184,... | collective-permute-start | bytes 61448 | tf_op jit(solution)/shard_map/ppermute | solution.py:307
  68.2 2.1 %inner_gradients.1 = (bf16[4,256,128]{2,1,0:T(8,128)(2,1)}, bf16[4,256,128]{2,1,0:T(8,128)(2,1)}, f32[4,256,128]{2,1,0:T(8,128)S(1)}, f32[4,256,128]{2,1,0:T(8,128)S(1)}) custom-call(bf16[4,256,128]{2,1,0:T(8,128)(2,1)S(1)} %copy-done.2, bf16[4,256,128]{2,1,0:T(8,128)(2,1)S(1)} %copy-done, bf16[4,256,128]{2,1,0:T(8,128)(2,1)S(1)} %copy-done.1, ...), custom_call_target="tpu_custom_call" | custom-call | flops 301989888 | bytes 4325376 | tf_op jit(solution)/shard_map/inner_gradients/pallas_call | solution.py:33
  70.3 3.6 %collective-permute-done.1.near_ref = f32[40,128]{1,0:T(8,128)S(1)} collective-permute-done((f32[40,128]{1,0:T(8,128)S(1)}, f32[40,128]{1,0:T(8,128)S(1)}, u32[]{:S(2)}, u32[]{:S(2)}) %collective-permute-start.1) | collective-permute-done | bytes 20512 | tf_op jit(solution)/shard_map/ppermute | solution.py:307
  73.9 0.1 backward_scan.1
  74.0 15.2 %all_to_all.29.back_ref = f32[16,32,128]{2,1,0:T(8,128)S(1)} all-to-all(f32[16,32,128]{2,1,0:T(8,128)S(1)} %backward_scan.1), channel_id=1, replica_groups={{0,8,16,24,32,40,48,56,64,72,80,88,96,104,112,120},{160,168,176,184,192..., dimensions={0} | all-to-all | bytes 524288 | tf_op jit(solution)/shard_map/all_to_all | solution.py:299
  89.1 1.1 %outer_gradients.1 = (bf16[4,256,128]{2,1,0:T(8,128)(2,1)}, bf16[4,256,128]{2,1,0:T(8,128)(2,1)}) custom-call(bf16[4,256,128]{2,1,0:T(8,128)(2,1)S(1)} %copy-done, bf16[4,256,128]{2,1,0:T(8,128)(2,1)S(1)} %copy-done.1, f32[4,256,128]{2,1,0:T(8,128)S(1)} %get-tuple-element.47.ki_ref, f32[4,256,128]{2,1,0:T(8,128)S(1)} %get-tuple-element.48.vi_ref, ...), custom_call_target="tpu_custom_call" | custom-call | flops 67108864 | bytes 2490368 | tf_op jit(solution)/shard_map/outer_gradients/pallas_call | solution.py:33
  (1 shorter events, 0.0 us)
Async XLA Ops:
  2.1 25.4 %copy-start.1 = (bf16[4,256,128]{2,1,0:T(8,128)(2,1)S(1)}, bf16[4,256,128]{2,1,0:T(8,128)(2,1)}, u32[]{:S(2)}) copy-start(bf16[4,256,128]{2,1,0:T(8,128)(2,1)} %v_ref.5) | copy-start | bytes 786436
  2.1 25.4 %copy-start.2 = (bf16[4,256,128]{2,1,0:T(8,128)(2,1)S(1)}, bf16[4,256,128]{2,1,0:T(8,128)(2,1)}, u32[]{:S(2)}) copy-start(bf16[4,256,128]{2,1,0:T(8,128)(2,1)} %q_ref.5) | copy-start | bytes 786436
  26.0 1.5 %copy-start = (bf16[4,256,128]{2,1,0:T(8,128)(2,1)S(1)}, bf16[4,256,128]{2,1,0:T(8,128)(2,1)}, u32[]{:S(2)}) copy-start(bf16[4,256,128]{2,1,0:T(8,128)(2,1)} %k_ref.5) | copy-start | bytes 786436
  26.2 2.8 %collective-permute-start = (f32[40,128]{1,0:T(8,128)S(1)}, f32[40,128]{1,0:T(8,128)S(1)}, u32[]{:S(2)}, u32[]{:S(2)}) collective-permute-start(f32[40,128]{1,0:T(8,128)S(1)} %get-tuple-element.32), channel_id=1, source_target_pairs={{0,128},{8,136},{16,144},{24,152},{32,160},{40,168},{48,176},{56,1... | collective-permute-start | bytes 61448 | tf_op jit(solution)/shard_map/ppermute | solution.py:307
  29.0 13.2 %copy-start.3 = (bf16[4,256,128]{2,1,0:T(8,128)(2,1)S(1)}, bf16[4,256,128]{2,1,0:T(8,128)(2,1)}, u32[]{:S(2)}) copy-start(bf16[4,256,128]{2,1,0:T(8,128)(2,1)} %g_ref.3) | copy-start | bytes 786436
  66.9 7.0 %collective-permute-start.1 = (f32[40,128]{1,0:T(8,128)S(1)}, f32[40,128]{1,0:T(8,128)S(1)}, u32[]{:S(2)}, u32[]{:S(2)}) collective-permute-start(f32[40,128]{1,0:T(8,128)S(1)} %backward_row.1), channel_id=1, source_target_pairs={{128,0},{136,8},{144,16},{152,24},{160,32},{168,40},{176,48},{184,... | collective-permute-start | bytes 61448 | tf_op jit(solution)/shard_map/ppermute | solution.py:307

commit v6 on v5

--- a/solution.py
+++ b/solution.py
@@ -10,6 +10,7 @@
 EPSILON = 1e-06
 ROW = 16
 LEAD = 4
+LATER = 4
 META = 8
 HIGH = lax.Precision.HIGHEST
 
@@ -18,6 +19,10 @@
     return lax.dot_general(
         a, b, (((da,), (db,)), ((), ())), preferred_element_type=jnp.float32
     )
+
+
+def later(member):
+    return (member + ROW - LATER) % ROW
 
 
 def listed():
@@ -133,11 +138,10 @@
 
 
 def backward_row(got_ref, fact_ref, sum_ref):
-    slot = listed()
-    state, mark = got_ref[slot(ROW - 1)], facts_of(fact_ref, ROW - 1)[1]
+    state, mark = got_ref[later(ROW - 1)], facts_of(fact_ref, ROW - 1)[1]
     for j in range(ROW - 2, -1, -1):
         decay, first, _ = facts_of(fact_ref, j)
-        state = jnp.where(mark == first, jnp.exp(decay), 0.0) * state + got_ref[slot(j)]
+        state = jnp.where(mark == first, jnp.exp(decay), 0.0) * state + got_ref[later(j)]
         mark = first
     summary(sum_ref, state, mark)
 
@@ -148,7 +152,7 @@
     state, mark = near_ref[0:depth], near_ref[depth + 1 : depth + 2]
     for j in range(ROW):
         decay, first, last = facts_of(fact_ref, j)
-        out_ref[slot(j)] = jnp.where(mark == first, state, 0.0)
+        out_ref[later(j)] = jnp.where(mark == first, state, 0.0)
         kept = jnp.where(mark == last, jnp.exp(decay), 0.0)
         state = kept * state + got_ref[pl.ds(slot(j) * (depth + 1), depth)]
         mark = last
@@ -156,18 +160,17 @@
 
 def backward_scan(got_ref, fact_ref, near_ref, out_ref):
     depth = out_ref.shape[1]
-    slot = listed()
     state, mark = near_ref[0:depth], near_ref[depth + 1 : depth + 2]
     for j in range(ROW - 1, -1, -1):
         decay, first, last = facts_of(fact_ref, j)
-        out_ref[slot(j)] = jnp.where(mark == last, state, 0.0)
-        state = jnp.where(mark == first, jnp.exp(decay), 0.0) * state + got_ref[slot(j)]
+        out_ref[later(j)] = jnp.where(mark == last, state, 0.0)
+        state = jnp.where(mark == first, jnp.exp(decay), 0.0) * state + got_ref[later(j)]
         mark = first
 
 
-def head_state(state_ref, slot, heads, h):
+def head_state(state_ref, heads, h):
     per_head = ROW // heads
-    slices = [state_ref[slot(h * per_head + part)] for part in range(per_head)]
+    slices = [state_ref[later(h * per_head + part)] for part in range(per_head)]
     return jnp.concatenate(slices, axis=0).astype(jnp.bfloat16)
 
 
@@ -197,10 +200,9 @@
 
 def attend(q_ref, g_ref, state_ref, within_ref, cols_ref, att_ref, sums_ref):
     heads, tokens, width = q_ref.shape
-    slot = listed()
     squares = crossed = jnp.zeros((tokens, width), jnp.float32)
     for h in range(heads):
-        state = head_state(state_ref, slot, heads, h)
+        state = head_state(state_ref, heads, h)
         enter = cols_ref[:, heads + h : heads + h + 1]
         att = within_ref[h] + dot(q_ref[h], state, 1, 0) * enter
         att_ref[h] = att
@@ -222,7 +224,6 @@
     heads, _, width = g_ref.shape
     per_head = ROW // heads
     depth = width // per_head
-    slot = listed()
     half = sums_ref.shape[1] // 2
     sums = jnp.sum(sums_ref[...], axis=0)
     root = jnp.sqrt(sums[:half] / features + EPSILON)
@@ -239,7 +240,7 @@
         ga_ref[h] = ga
         back = dot(decayed_ref[h], ga, 1, 0)
         for part in range(per_head):
-            pay_ref[slot(h * per_head + part)] = back[part * depth : (part + 1) * depth]
+            pay_ref[later(h * per_head + part)] = back[part * depth : (part + 1) * depth]
 
 
 def inner_gradients(
@@ -259,14 +260,13 @@
     vi_ref,
 ):
     heads = q_ref.shape[0]
-    slot = listed()
     for h in range(heads):
         norm_ref[h] = (att_ref[h] * scale_ref[...]).astype(jnp.bfloat16)
         ga = ga_ref[h]
         decays = decays_of(rows_ref, cols_ref, heads, h)
         slope = (dot(ga, v_ref[h], 1, 1) * decays).astype(jnp.bfloat16)
         enter = cols_ref[:, heads + h : heads + h + 1]
-        state = head_state(state_ref, slot, heads, h)
+        state = head_state(state_ref, heads, h)
         gq_ref[h] = (dot(slope, k_ref[h], 1, 0) + dot(ga, state, 1, 1) * enter).astype(jnp.bfloat16)
         ki_ref[h] = dot(slope, q_ref[h], 0, 0)
         vi_ref[h] = dot(scores_ref[h], ga, 0, 0)
@@ -276,10 +276,9 @@
     k_ref, v_ref, ki_ref, vi_ref, back_ref, cols_ref, gk_hbm, gv_hbm, gk_ref, gv_ref, sems
 ):
     heads = k_ref.shape[0]
-    slot = listed()
     copies = []
     for h in range(heads):
-        back = head_state(back_ref, slot, heads, h)
+        back = head_state(back_ref, heads, h)
         leave = cols_ref[:, 2 * heads + h : 2 * heads + h + 1]
         gk_ref[h] = (ki_ref[h] + dot(v_ref[h], back, 1, 1) * leave).astype(jnp.bfloat16)
         copies.append(pltpu.make_async_copy(gk_ref.at[h], gk_hbm.at[h], sems.at[2 * h]))
@@ -311,9 +310,9 @@
     heads, tokens, width = query_rows.shape
     depth = heads * width // ROW
     devices = lax.axis_size("seq")
-    groups = [
-        [at + (i + (LEAD if at else 0)) % ROW for i in range(ROW)] for at in range(0, devices, ROW)
-    ]
+    starts = range(0, devices, ROW)
+    first = [[at + (i + (LEAD if at else 0)) % ROW for i in range(ROW)] for at in starts]
+    groups = [[at + (i + LATER) % ROW for i in range(ROW)] for at in starts]
     f32, bf16 = jnp.float32, jnp.bfloat16
     block = (heads, tokens, width)
     product = 2 * heads * tokens * width * width
@@ -337,7 +336,7 @@
         from_hbm=True,
     )(*map(in_hbm, (log_gate, episode.reshape(1, tokens), key_rows, value_rows)))
     dense = (ROW, depth + 1, 1, width)
-    got = exchange(pay.reshape(dense), groups).reshape(pay.shape)
+    got = exchange(pay.reshape(dense), first).reshape(pay.shape)
     total, facts = call(
         forward_row, [((depth + META, width), f32), ((ROW, META, width), f32)], got.size
     )(got)
@@ -361,7 +360,10 @@
     attention, sums = call(attend, [(block, f32), ((across, lines, width), f32)], product)(
         query_rows, grad_out, state, within, cols
     )
-    sums = lax.all_to_all(sums, "head", split_axis=0, concat_axis=0, tiled=True)
+    order = [[(i + across - 2) % across for i in range(across)]]
+    sums = lax.all_to_all(
+        sums, "head", split_axis=0, concat_axis=0, tiled=True, axis_index_groups=order
+    )
     features = heads * across * width
     grad_attn, pay, scale = call(
         functools.partial(own_gradient_state, features),

time: 90.6 us -> 88.6 us (0.978)
  the two profiles are of different devices: /device:TPU:8 before, /device:TPU:1 now
where the time goes in v6:
time: 88.6 us; the launch traced here: 88.2 us
  blocking collectives  71 us (80%)
  starting transfers between devices  6.61 us (7%)
  Pallas kernels  6.59 us (7%)
  waiting for transfers between devices  3.19 us (4%)
    all_to_all x4, blocking collectives, exchange(): lax.all_to_all(block, 'seq', split_axis=0, concat_axis=0, tiled=True, axi...  58 us
    all_to_all x1, blocking collectives, per_device(): lax.all_to_all(sums, 'head', split_axis=0, concat_axis=0, tiled=True, axi...  13 us
    ppermute x2, starting transfers between devices, passed_along(): return lax.ppermute(block, 'seq', route)  6.61 us
    pallas_call x10, Pallas kernels, run(): pl.pallas_call(body, out_shape=shapes, in_specs=[pl.BlockSpec(memory_spac...  6.59 us
    ppermute x2, waiting for transfers between devices, passed_along(): return lax.ppermute(block, 'seq', route)  3.19 us
  transfers between devices with their start and end apart: 2, of which 2 were waited for; matrix products, arithmetic and copies ran while one was open for 0% of the time, Pallas kernels for 3%

profile of v6, /device:TPU:1, one launch (start us, length us, event | category | flops | bytes accessed | tf_op | source)
XLA Modules:
  0.0 88.2 jit_solution(14947017147864412059)
XLA Ops:
  0.6 1.5 %local_states.1 = (f32[528,128]{1,0:T(8,128)S(1)}, f32[128,256]{1,0:T(8,128)S(1)}) custom-call(f32[4,256]{1,0:T(4,128)} %gate_hbm.1, s32[1,256]{1,0:T(1,128)} %bitcast.6, bf16[4,256,128]{2,1,0:T(8,128)(2,1)} %k_ref.5, bf16[4,256,128]{2,1,0:T(8,128)(2,1)} %v_ref.5), custom_call_target="tpu_custom_call" | custom-call | flops 33554432 | bytes 930816 | tf_op jit(solution)/shard_map/local_states/pallas_call | solution.py:38
  2.1 0.0 copy-start.1
  2.1 0.0 copy-start.2
  2.1 17.2 %all_to_all.25 = f32[16,33,1,128]{3,2,1,0:T(1,128)S(1)} all-to-all(f32[16,33,1,128]{3,2,1,0:T(1,128)S(1)} %bitcast.5), channel_id=1, replica_groups={{0,8,16,24,32,40,48,56,64,72,80,88,96,104,112,120},{160,168,176,184,192..., dimensions={0} | all-to-all | bytes 540672 | tf_op jit(solution)/shard_map/all_to_all | solution.py:298
  19.3 0.0 copy-start
  19.3 0.2 forward_row.1
  19.5 5.3 %collective-permute-start = (f32[40,128]{1,0:T(8,128)S(1)}, f32[40,128]{1,0:T(8,128)S(1)}, u32[]{:S(2)}, u32[]{:S(2)}) collective-permute-start(f32[40,128]{1,0:T(8,128)S(1)} %get-tuple-element.32), channel_id=1, source_target_pairs={{0,128},{8,136},{16,144},{24,152},{32,160},{40,168},{48,176},{56,1... | collective-permute-start | bytes 61448 | tf_op jit(solution)/shard_map/ppermute | solution.py:306
  24.8 0.0 copy-done.1
  24.8 0.0 copy-done.2
  24.8 0.0 copy-done
  24.8 0.7 within_stretch.1
  25.6 0.1 collective-permute-done.near_ref
  25.7 0.1 forward_scan.1
  25.8 0.0 copy-start.3
  25.8 12.4 %all_to_all.26.state_ref = f32[16,32,128]{2,1,0:T(8,128)S(1)} all-to-all(f32[16,32,128]{2,1,0:T(8,128)S(1)} %forward_scan.1), channel_id=1, replica_groups={{32,40,48,56,64,72,80,88,96,104,112,120,0,8,16,24},{160,168,176,184,192..., dimensions={0} | all-to-all | bytes 524288 | tf_op jit(solution)/shard_map/all_to_all | solution.py:298
  38.2 0.0 copy-done.3
  38.2 0.4 attend.1
  38.6 13.0 %all_to_all.27.sums_ref = f32[8,4,128]{2,1,0:T(4,128)S(1)} all-to-all(f32[8,4,128]{2,1,0:T(4,128)S(1)} %get-tuple-element.38), channel_id=1, replica_groups={{6,7,0,1,2,3,4,5},{14,15,8,9,10,11,12,13},{22,23,16,17,18,19,20,21},{30..., dimensions={0} | all-to-all | bytes 32768 | tf_op jit(solution)/shard_map/all_to_all | solution.py:364
  51.6 0.5 own_gradient_state.1
  52.1 13.9 %all_to_all.28.got_ref = f32[16,32,128]{2,1,0:T(8,128)S(1)} all-to-all(f32[16,32,128]{2,1,0:T(8,128)S(1)} %get-tuple-element.44), channel_id=1, replica_groups={{32,40,48,56,64,72,80,88,96,104,112,120,0,8,16,24},{160,168,176,184,192..., dimensions={0} | all-to-all | bytes 524288 | tf_op jit(solution)/shard_map/all_to_all | solution.py:298
  66.0 1.3 %collective-permute-start.1 = (f32[40,128]{1,0:T(8,128)S(1)}, f32[40,128]{1,0:T(8,128)S(1)}, u32[]{:S(2)}, u32[]{:S(2)}) collective-permute-start(f32[40,128]{1,0:T(8,128)S(1)} %backward_row.1), channel_id=1, source_target_pairs={{128,0},{136,8},{144,16},{152,24},{160,32},{168,40},{176,48},{184,... | collective-permute-start | bytes 61448 | tf_op jit(solution)/shard_map/ppermute | solution.py:306
  67.3 2.1 %inner_gradients.1 = (bf16[4,256,128]{2,1,0:T(8,128)(2,1)}, bf16[4,256,128]{2,1,0:T(8,128)(2,1)}, f32[4,256,128]{2,1,0:T(8,128)S(1)}, f32[4,256,128]{2,1,0:T(8,128)S(1)}) custom-call(bf16[4,256,128]{2,1,0:T(8,128)(2,1)S(1)} %copy-done.2, bf16[4,256,128]{2,1,0:T(8,128)(2,1)S(1)} %copy-done, bf16[4,256,128]{2,1,0:T(8,128)(2,1)S(1)} %copy-done.1, ...), custom_call_target="tpu_custom_call" | custom-call | flops 301989888 | bytes 4325376 | tf_op jit(solution)/shard_map/inner_gradients/pallas_call | solution.py:38
  69.5 3.1 %collective-permute-done.1.near_ref = f32[40,128]{1,0:T(8,128)S(1)} collective-permute-done((f32[40,128]{1,0:T(8,128)S(1)}, f32[40,128]{1,0:T(8,128)S(1)}, u32[]{:S(2)}, u32[]{:S(2)}) %collective-permute-start.1) | collective-permute-done | bytes 20512 | tf_op jit(solution)/shard_map/ppermute | solution.py:306
  72.6 14.5 %all_to_all.29.back_ref = f32[16,32,128]{2,1,0:T(8,128)S(1)} all-to-all(f32[16,32,128]{2,1,0:T(8,128)S(1)} %backward_scan.1), channel_id=1, replica_groups={{32,40,48,56,64,72,80,88,96,104,112,120,0,8,16,24},{160,168,176,184,192..., dimensions={0} | all-to-all | bytes 524288 | tf_op jit(solution)/shard_map/all_to_all | solution.py:298
  87.1 1.0 %outer_gradients.1 = (bf16[4,256,128]{2,1,0:T(8,128)(2,1)}, bf16[4,256,128]{2,1,0:T(8,128)(2,1)}) custom-call(bf16[4,256,128]{2,1,0:T(8,128)(2,1)S(1)} %copy-done, bf16[4,256,128]{2,1,0:T(8,128)(2,1)S(1)} %copy-done.1, f32[4,256,128]{2,1,0:T(8,128)S(1)} %get-tuple-element.47.ki_ref, f32[4,256,128]{2,1,0:T(8,128)S(1)} %get-tuple-element.48.vi_ref, ...), custom_call_target="tpu_custom_call" | custom-call | flops 67108864 | bytes 2490368 | tf_op jit(solution)/shard_map/outer_gradients/pallas_call | solution.py:38
  (2 shorter events, 0.1 us)
Async XLA Ops:
  2.1 22.7 %copy-start.1 = (bf16[4,256,128]{2,1,0:T(8,128)(2,1)S(1)}, bf16[4,256,128]{2,1,0:T(8,128)(2,1)}, u32[]{:S(2)}) copy-start(bf16[4,256,128]{2,1,0:T(8,128)(2,1)} %v_ref.5) | copy-start | bytes 786436
  2.1 22.7 %copy-start.2 = (bf16[4,256,128]{2,1,0:T(8,128)(2,1)S(1)}, bf16[4,256,128]{2,1,0:T(8,128)(2,1)}, u32[]{:S(2)}) copy-start(bf16[4,256,128]{2,1,0:T(8,128)(2,1)} %q_ref.5) | copy-start | bytes 786436
  19.3 5.5 %copy-start = (bf16[4,256,128]{2,1,0:T(8,128)(2,1)S(1)}, bf16[4,256,128]{2,1,0:T(8,128)(2,1)}, u32[]{:S(2)}) copy-start(bf16[4,256,128]{2,1,0:T(8,128)(2,1)} %k_ref.5) | copy-start | bytes 786436
  19.5 6.2 %collective-permute-start = (f32[40,128]{1,0:T(8,128)S(1)}, f32[40,128]{1,0:T(8,128)S(1)}, u32[]{:S(2)}, u32[]{:S(2)}) collective-permute-start(f32[40,128]{1,0:T(8,128)S(1)} %get-tuple-element.32), channel_id=1, source_target_pairs={{0,128},{8,136},{16,144},{24,152},{32,160},{40,168},{48,176},{56,1... | collective-permute-start | bytes 61448 | tf_op jit(solution)/shard_map/ppermute | solution.py:306
  25.8 12.4 %copy-start.3 = (bf16[4,256,128]{2,1,0:T(8,128)(2,1)S(1)}, bf16[4,256,128]{2,1,0:T(8,128)(2,1)}, u32[]{:S(2)}) copy-start(bf16[4,256,128]{2,1,0:T(8,128)(2,1)} %g_ref.3) | copy-start | bytes 786436
  66.0 6.5 %collective-permute-start.1 = (f32[40,128]{1,0:T(8,128)S(1)}, f32[40,128]{1,0:T(8,128)S(1)}, u32[]{:S(2)}, u32[]{:S(2)}) collective-permute-start(f32[40,128]{1,0:T(8,128)S(1)} %backward_row.1), channel_id=1, source_target_pairs={{128,0},{136,8},{144,16},{152,24},{160,32},{168,40},{176,48},{184,... | collective-permute-start | bytes 61448 | tf_op jit(solution)/shard_map/ppermute | solution.py:306

commit v7 on v6

--- a/solution.py
+++ b/solution.py
@@ -360,7 +360,7 @@
     attention, sums = call(attend, [(block, f32), ((across, lines, width), f32)], product)(
         query_rows, grad_out, state, within, cols
     )
-    order = [[(i + across - 2) % across for i in range(across)]]
+    order = [[(i + across - 4) % across for i in range(across)]]
     sums = lax.all_to_all(
         sums, "head", split_axis=0, concat_axis=0, tiled=True, axis_index_groups=order
     )

time: 88.6 us -> 87.8 us (level)
  no operation moved by 1% of the time
where the time goes in v7:
time: 87.8 us; the launch traced here: 87.4 us
  blocking collectives  70.4 us (80%)
  starting transfers between devices  6.61 us (8%)
  Pallas kernels  6.6 us (8%)
  waiting for transfers between devices  3.03 us (3%)
    all_to_all x4, blocking collectives, exchange(): lax.all_to_all(block, 'seq', split_axis=0, concat_axis=0, tiled=True, axi...  58 us
    all_to_all x1, blocking collectives, per_device(): lax.all_to_all(sums, 'head', split_axis=0, concat_axis=0, tiled=True, axi...  12.4 us
    ppermute x2, starting transfers between devices, passed_along(): return lax.ppermute(block, 'seq', route)  6.61 us
    pallas_call x10, Pallas kernels, run(): pl.pallas_call(body, out_shape=shapes, in_specs=[pl.BlockSpec(memory_spac...  6.6 us
    ppermute x2, waiting for transfers between devices, passed_along(): return lax.ppermute(block, 'seq', route)  3.03 us
  transfers between devices with their start and end apart: 2, of which 2 were waited for; matrix products, arithmetic and copies ran while one was open for 0% of the time, Pallas kernels for 3%

profile of v7, /device:TPU:1, one launch (start us, length us, event | category | flops | bytes accessed | tf_op | source)
XLA Modules:
  0.0 87.4 jit_solution(11096218569063226635)
XLA Ops:
  0.6 1.5 %local_states.1 = (f32[528,128]{1,0:T(8,128)S(1)}, f32[128,256]{1,0:T(8,128)S(1)}) custom-call(f32[4,256]{1,0:T(4,128)} %gate_hbm.1, s32[1,256]{1,0:T(1,128)} %bitcast.6, bf16[4,256,128]{2,1,0:T(8,128)(2,1)} %k_ref.5, bf16[4,256,128]{2,1,0:T(8,128)(2,1)} %v_ref.5), custom_call_target="tpu_custom_call" | custom-call | flops 33554432 | bytes 930816 | tf_op jit(solution)/shard_map/local_states/pallas_call | solution.py:38
  2.1 0.0 copy-start.1
  2.1 0.0 copy-start.2
  2.1 17.2 %all_to_all.25 = f32[16,33,1,128]{3,2,1,0:T(1,128)S(1)} all-to-all(f32[16,33,1,128]{3,2,1,0:T(1,128)S(1)} %bitcast.5), channel_id=1, replica_groups={{0,8,16,24,32,40,48,56,64,72,80,88,96,104,112,120},{160,168,176,184,192..., dimensions={0} | all-to-all | bytes 540672 | tf_op jit(solution)/shard_map/all_to_all | solution.py:298
  19.3 0.0 copy-start
  19.3 0.2 forward_row.1
  19.5 5.3 %collective-permute-start = (f32[40,128]{1,0:T(8,128)S(1)}, f32[40,128]{1,0:T(8,128)S(1)}, u32[]{:S(2)}, u32[]{:S(2)}) collective-permute-start(f32[40,128]{1,0:T(8,128)S(1)} %get-tuple-element.32), channel_id=1, source_target_pairs={{0,128},{8,136},{16,144},{24,152},{32,160},{40,168},{48,176},{56,1... | collective-permute-start | bytes 61448 | tf_op jit(solution)/shard_map/ppermute | solution.py:306
  24.8 0.0 copy-done.1
  24.8 0.0 copy-done.2
  24.8 0.0 copy-done
  24.8 0.7 within_stretch.1
  25.6 0.1 collective-permute-done.near_ref
  25.7 0.1 forward_scan.1
  25.8 0.0 copy-start.3
  25.8 12.4 %all_to_all.26.state_ref = f32[16,32,128]{2,1,0:T(8,128)S(1)} all-to-all(f32[16,32,128]{2,1,0:T(8,128)S(1)} %forward_scan.1), channel_id=1, replica_groups={{32,40,48,56,64,72,80,88,96,104,112,120,0,8,16,24},{160,168,176,184,192..., dimensions={0} | all-to-all | bytes 524288 | tf_op jit(solution)/shard_map/all_to_all | solution.py:298
  38.2 0.0 copy-done.3
  38.2 0.4 attend.1
  38.6 12.4 %all_to_all.27.sums_ref = f32[8,4,128]{2,1,0:T(4,128)S(1)} all-to-all(f32[8,4,128]{2,1,0:T(4,128)S(1)} %get-tuple-element.38), channel_id=1, replica_groups={{4,5,6,7,0,1,2,3},{12,13,14,15,8,9,10,11},{20,21,22,23,16,17,18,19},{28..., dimensions={0} | all-to-all | bytes 32768 | tf_op jit(solution)/shard_map/all_to_all | solution.py:364
  51.0 0.5 own_gradient_state.1
  51.5 13.9 %all_to_all.28.got_ref = f32[16,32,128]{2,1,0:T(8,128)S(1)} all-to-all(f32[16,32,128]{2,1,0:T(8,128)S(1)} %get-tuple-element.44), channel_id=1, replica_groups={{32,40,48,56,64,72,80,88,96,104,112,120,0,8,16,24},{160,168,176,184,192..., dimensions={0} | all-to-all | bytes 524288 | tf_op jit(solution)/shard_map/all_to_all | solution.py:298
  65.4 1.3 %collective-permute-start.1 = (f32[40,128]{1,0:T(8,128)S(1)}, f32[40,128]{1,0:T(8,128)S(1)}, u32[]{:S(2)}, u32[]{:S(2)}) collective-permute-start(f32[40,128]{1,0:T(8,128)S(1)} %backward_row.1), channel_id=1, source_target_pairs={{128,0},{136,8},{144,16},{152,24},{160,32},{168,40},{176,48},{184,... | collective-permute-start | bytes 61448 | tf_op jit(solution)/shard_map/ppermute | solution.py:306
  66.7 2.1 %inner_gradients.1 = (bf16[4,256,128]{2,1,0:T(8,128)(2,1)}, bf16[4,256,128]{2,1,0:T(8,128)(2,1)}, f32[4,256,128]{2,1,0:T(8,128)S(1)}, f32[4,256,128]{2,1,0:T(8,128)S(1)}) custom-call(bf16[4,256,128]{2,1,0:T(8,128)(2,1)S(1)} %copy-done.2, bf16[4,256,128]{2,1,0:T(8,128)(2,1)S(1)} %copy-done, bf16[4,256,128]{2,1,0:T(8,128)(2,1)S(1)} %copy-done.1, ...), custom_call_target="tpu_custom_call" | custom-call | flops 301989888 | bytes 4325376 | tf_op jit(solution)/shard_map/inner_gradients/pallas_call | solution.py:38
  68.8 2.9 %collective-permute-done.1.near_ref = f32[40,128]{1,0:T(8,128)S(1)} collective-permute-done((f32[40,128]{1,0:T(8,128)S(1)}, f32[40,128]{1,0:T(8,128)S(1)}, u32[]{:S(2)}, u32[]{:S(2)}) %collective-permute-start.1) | collective-permute-done | bytes 20512 | tf_op jit(solution)/shard_map/ppermute | solution.py:306
  71.8 14.5 %all_to_all.29.back_ref = f32[16,32,128]{2,1,0:T(8,128)S(1)} all-to-all(f32[16,32,128]{2,1,0:T(8,128)S(1)} %backward_scan.1), channel_id=1, replica_groups={{32,40,48,56,64,72,80,88,96,104,112,120,0,8,16,24},{160,168,176,184,192..., dimensions={0} | all-to-all | bytes 524288 | tf_op jit(solution)/shard_map/all_to_all | solution.py:298
  86.3 1.0 %outer_gradients.1 = (bf16[4,256,128]{2,1,0:T(8,128)(2,1)}, bf16[4,256,128]{2,1,0:T(8,128)(2,1)}) custom-call(bf16[4,256,128]{2,1,0:T(8,128)(2,1)S(1)} %copy-done, bf16[4,256,128]{2,1,0:T(8,128)(2,1)S(1)} %copy-done.1, f32[4,256,128]{2,1,0:T(8,128)S(1)} %get-tuple-element.47.ki_ref, f32[4,256,128]{2,1,0:T(8,128)S(1)} %get-tuple-element.48.vi_ref, ...), custom_call_target="tpu_custom_call" | custom-call | flops 67108864 | bytes 2490368 | tf_op jit(solution)/shard_map/outer_gradients/pallas_call | solution.py:38
  (2 shorter events, 0.1 us)
Async XLA Ops:
  2.1 22.7 %copy-start.1 = (bf16[4,256,128]{2,1,0:T(8,128)(2,1)S(1)}, bf16[4,256,128]{2,1,0:T(8,128)(2,1)}, u32[]{:S(2)}) copy-start(bf16[4,256,128]{2,1,0:T(8,128)(2,1)} %v_ref.5) | copy-start | bytes 786436
  2.1 22.7 %copy-start.2 = (bf16[4,256,128]{2,1,0:T(8,128)(2,1)S(1)}, bf16[4,256,128]{2,1,0:T(8,128)(2,1)}, u32[]{:S(2)}) copy-start(bf16[4,256,128]{2,1,0:T(8,128)(2,1)} %q_ref.5) | copy-start | bytes 786436
  19.3 5.5 %copy-start = (bf16[4,256,128]{2,1,0:T(8,128)(2,1)S(1)}, bf16[4,256,128]{2,1,0:T(8,128)(2,1)}, u32[]{:S(2)}) copy-start(bf16[4,256,128]{2,1,0:T(8,128)(2,1)} %k_ref.5) | copy-start | bytes 786436
  19.5 6.2 %collective-permute-start = (f32[40,128]{1,0:T(8,128)S(1)}, f32[40,128]{1,0:T(8,128)S(1)}, u32[]{:S(2)}, u32[]{:S(2)}) collective-permute-start(f32[40,128]{1,0:T(8,128)S(1)} %get-tuple-element.32), channel_id=1, source_target_pairs={{0,128},{8,136},{16,144},{24,152},{32,160},{40,168},{48,176},{56,1... | collective-permute-start | bytes 61448 | tf_op jit(solution)/shard_map/ppermute | solution.py:306
  25.8 12.4 %copy-start.3 = (bf16[4,256,128]{2,1,0:T(8,128)(2,1)S(1)}, bf16[4,256,128]{2,1,0:T(8,128)(2,1)}, u32[]{:S(2)}) copy-start(bf16[4,256,128]{2,1,0:T(8,128)(2,1)} %g_ref.3) | copy-start | bytes 786436
  65.4 6.3 %collective-permute-start.1 = (f32[40,128]{1,0:T(8,128)S(1)}, f32[40,128]{1,0:T(8,128)S(1)}, u32[]{:S(2)}, u32[]{:S(2)}) collective-permute-start(f32[40,128]{1,0:T(8,128)S(1)} %backward_row.1), channel_id=1, source_target_pairs={{128,0},{136,8},{144,16},{152,24},{160,32},{168,40},{176,48},{184,... | collective-permute-start | bytes 61448 | tf_op jit(solution)/shard_map/ppermute | solution.py:306
